TPU v7x, 32 devices: a whole 2x2x4 slice. The times are simulated.
32 devices in a mesh: grp: 4 (over y, core), rep: 2 (over x), mp: 4 (over z).
Axes of the slice: x: 2, y: 2, z: 4, core: 2. Of those that a mesh axis runs over, the one named last changes fastest.
Arguments:
- inputs: bfloat16 [16, 8192], P('grp', 'rep'), may hold values from -6 to 6
- stale_rows: int32 [16], P('grp'), may hold values 0 or 1
- row_order: int32 [16], P('grp'), may hold values from 0 to 3, as said below
- lengths: int32 [16], P(('grp', 'rep')), may hold values from 2 to 1024
- old_q: bfloat16 [8192, 64, 128], P('rep', 'mp'), may hold values from -0.0625 to 0.0625
- old_kv: bfloat16 [8192, 16, 128], P('rep', 'mp'), may hold values from -0.0625 to 0.0625
- fresh_q: bfloat16 [8192, 64, 128], P('rep', 'mp', 'grp'), may hold values from -0.0625 to 0.0625
- fresh_kv: bfloat16 [8192, 16, 128], P('rep', 'mp', 'grp'), may hold values from -0.0625 to 0.0625
- key_cache: bfloat16 [16, 1024, 8, 128], P(('grp', 'rep'), 'mp'), may hold values from -320 to 320
- value_cache: bfloat16 [16, 1024, 8, 128], P(('grp', 'rep'), 'mp'), may hold values from -6 to 6
Outputs:
- attention: bfloat16 [16, 64, 128], P(('grp', 'rep'), 'mp')
Inputs may be any that keep to these rules, and one draw needn't show every extreme that they name: `row_order`: within each group of 4 consecutive entries, a permutation of 0 to 3; entry i names the cache row of the group's i-th shortest row by lengths, ties by cache row.
All inputs are finite; a program needn't handle non-finite values. No bound on the sum of `stale_rows` on one device may be relied on, other than what follows from the above.
Results may differ from a plain program's by a relative error of at most 0.017.
Values may be sent and summed in bfloat16 or wider, within the bound.
No kernel may reach another device: no remote copies, remote signals or barrier semaphores. Data moves between devices by JAX's collectives and lax.ppermute only.
A program may use at most 128 MiB of HBM per device.

v0:
```python
import math

import jax
import jax.numpy as jnp
from jax import lax
from jax.sharding import PartitionSpec as P


def reduce_shards(exchanged):
    outs_in, tops_in, sums_in = exchanged
    joined = jnp.max(tops_in, axis=0)
    weights = jnp.exp(tops_in - joined[None])
    return (
        jnp.sum(outs_in * weights[..., None], axis=0),
        joined,
        jnp.sum(sums_in * weights, axis=0),
    )


def local(
    inputs, stale_rows, row_order, lengths, old_q, old_kv, fresh_q, fresh_kv, key_cache, value_cache
):
    group_rows, part_width = inputs.shape
    heads_here = old_q.shape[1]
    head_size = old_q.shape[2]
    inverse = jnp.argsort(row_order)
    slot_inputs = jnp.take(inputs, inverse, axis=0)
    slot_stale = jnp.take(stale_rows, inverse, axis=0)

    def project(weight):
        flat_weight = weight.reshape(part_width, weight.shape[1] * weight.shape[2])
        product = jnp.dot(slot_inputs, flat_weight, preferred_element_type=jnp.float32)
        return product.reshape(group_rows, weight.shape[1], weight.shape[2])

    fresh_queries = project(lax.all_gather(fresh_q, "grp", axis=2, tiled=True))
    refreshed_slot_list = project(lax.all_gather(fresh_kv, "grp", axis=2, tiled=True))
    choose_old = (slot_stale == 1)[:, None, None]
    query_terms = jnp.where(choose_old, project(old_q), fresh_queries)
    slot_terms = jnp.where(choose_old, project(old_kv), refreshed_slot_list)
    my_queries, my_slots = (
        lax.psum_scatter(query_terms, "rep", scatter_dimension=0, tiled=True),
        lax.psum_scatter(slot_terms, "rep", scatter_dimension=0, tiled=True),
    )
    my_queries = my_queries.astype(jnp.bfloat16)
    my_slots = my_slots.astype(jnp.bfloat16)
    all_queries, all_slots = (
        lax.all_gather(my_queries, "mp", axis=1, tiled=True),
        lax.all_gather(my_slots, "mp", axis=1, tiled=True),
    )
    rows_here = all_queries.shape[0]
    head_count = all_queries.shape[1]
    kv_heads = all_slots.shape[1] // 2
    per_group = head_count // kv_heads
    positions_here = key_cache.shape[1]
    rescale_multiplier = 1.0 / math.sqrt(head_size)
    grouped_query_rows = all_queries.reshape(rows_here, kv_heads, per_group, head_size)
    scores = (
        jnp.einsum(
            "bkgd,blkd->bkgl", grouped_query_rows, key_cache, preferred_element_type=jnp.float32
        )
        * rescale_multiplier
    )
    positions = lax.axis_index("mp") * positions_here + jnp.arange(positions_here, dtype=jnp.int32)
    allowed = (positions[None, :] < lengths[:, None])[:, None, None, :]
    local_top = jnp.max(jnp.where(allowed, scores, -1e30), axis=-1)
    probable = jnp.where(allowed, jnp.exp(scores - local_top[..., None]), 0.0)
    local_sum = jnp.sum(probable, axis=-1).reshape(rows_here, head_count)
    local_out = jnp.einsum(
        "bkgl,blkd->bkgd",
        probable.astype(jnp.bfloat16),
        value_cache,
        preferred_element_type=jnp.float32,
    ).reshape(rows_here, head_count, head_size)
    local_top = local_top.reshape(rows_here, head_count)
    head_output_vector, head_top, head_sum = reduce_shards(
        (
            lax.all_to_all(
                local_out[None].astype(jnp.bfloat16), "mp", split_axis=2, concat_axis=0, tiled=True
            ).astype(jnp.float32),
            lax.all_to_all(
                local_top[None].astype(jnp.bfloat16), "mp", split_axis=2, concat_axis=0, tiled=True
            ).astype(jnp.float32),
            lax.all_to_all(
                local_sum[None].astype(jnp.bfloat16), "mp", split_axis=2, concat_axis=0, tiled=True
            ).astype(jnp.float32),
        )
    )
    head_index = (
        lax.axis_index("mp") * heads_here + jnp.arange(heads_here, dtype=jnp.int32)
    ) // per_group
    incoming_keys = jnp.take(all_slots[:, :kv_heads], head_index, axis=1).astype(jnp.float32)
    new_values = jnp.take(all_slots[:, kv_heads:], head_index, axis=1).astype(jnp.float32)
    incoming_score = (
        jnp.sum(my_queries.astype(jnp.float32) * incoming_keys, axis=-1) * rescale_multiplier
    )
    joined = jnp.maximum(head_top, incoming_score)
    kept_share = jnp.exp(head_top - joined)
    new_weight = jnp.exp(incoming_score - joined)
    numerator = head_output_vector * kept_share[..., None] + new_weight[..., None] * new_values
    softmax_divisor = head_sum * kept_share + new_weight
    return (numerator / softmax_divisor[..., None]).astype(jnp.bfloat16)


def solution(mesh):
    return jax.shard_map(
        local,
        mesh=mesh,
        in_specs=(
            P("grp", "rep"),
            P("grp"),
            P("grp"),
            P(("grp", "rep")),
            P("rep", "mp", None),
            P("rep", "mp", None),
            P("rep", "mp", "grp"),
            P("rep", "mp", "grp"),
            P(("grp", "rep"), "mp", None, None),
            P(("grp", "rep"), "mp", None, None),
        ),
        out_specs=P(("grp", "rep"), "mp", None),
        check_vma=False,
    )
```

profile of v0, /device:TPU:0, one launch (start us, length us, event | category | flops | bytes accessed | tf_op | source)
XLA Modules:
  0.0 231.3 jit_solution(13891242941532655031)
XLA Ops:
  6.6 0.7 all-gather.5.cloned.1.call-update
  7.3 0.7 all-gather.3.cloned.1.call-update
  8.1 0.7 sort.17
  8.9 0.6 gather_fusion
  9.5 0.6 gather_fusion.1
  10.1 4.8 %copy.143 = bf16[512,8,4,128]{3,1,2,0:T(8,128)(2,1)} copy(bf16[512,8,4,128]{3,2,1,0:T(4,128)(2,1)} %bitcast.81) | data formatting | bytes 8388608
  14.9 6.5 %copy.108 = bf16[512,4096]{1,0:T(8,128)(2,1)} copy(bf16[512,4096]{0,1:T(8,128)(2,1)} %bitcast.80) | data formatting | bytes 8388608 | tf_op jit(solution)/shard_map/dot_general | solution.py:32
  21.4 17.2 %copy.142 = bf16[512,8,16,128]{3,1,2,0:T(8,128)(2,1)} copy(bf16[512,8,16,128]{3,2,1,0:T(8,128)(2,1)} %bitcast.78) | data formatting | bytes 33554432
  38.7 21.2 %copy.96 = bf16[2048,4096]{1,0:T(8,128)(2,1)} copy(bf16[2048,4096]{0,1:T(8,128)(2,1)} %bitcast.77) | data formatting | bytes 33554432 | tf_op jit(solution)/shard_map/dot_general | solution.py:32
  61.3 4.6 %fusion.19 = f32[4,4,128]{2,0,1:T(4,128)S(1)} fusion(bf16[4,128,4096]{2,1,0:T(8,128)(2,1)} %bitcast.79, bf16[4,4096]{1,0:T(4,128)(2,1)S(1)} %gather_fusion.1, pred[4]{0:T(512)(128)(4,1)S(1)} %get-tuple-element.16), kind=kOutput, calls=%fused_computation.28 | convolution fusion | flops 16793600 | bytes 4235268 | tf_op jit(solution)/shard_map/dot_general | solution.py:32
  65.9 3.6 %fusion.5 = f32[4,4,128]{2,0,1:T(4,128)S(1)} fusion(f32[4,4,128]{2,0,1:T(4,128)S(1)} %fusion.19, bf16[4096,4,128]{0,2,1:T(8,128)(2,1)} %all-gather.5.cloned.1.call-done, pred[4]{0:T(512)(128)(4,1)S(1)} %get-tuple-element.15, bf16[4,4096]{1,0:T(4,128)(2,1)S(1)} %gather_fusion.1, pred[4]{0:T(512)(128)(4,1)S(1)} %get-tuple-element.16), kind=kOutput, calls=%fused_computation.14 | convolution fusion | flops 16795648 | bytes 4243464 | tf_op jit(solution)/shard_map/dot_general | solution.py:32
  69.5 5.3 %all-reduce = bf16[4,4,128]{2,1,0:T(4,128)(2,1)S(1)} all-reduce(f32[4,4,128]{2,1,0:T(4,128)S(1)} %copy.109), channel_id=3, replica_groups=mesh['grp'=4,'rep'=2,'mp'=4] {'rep'}, use_global_device_ids=true, to_apply=%region_5.6.clone | all-reduce | flops 2048 | bytes 12288
  74.9 12.6 %all_gather.15 = bf16[2,16,128]{2,0,1:T(2,128)(2,1)S(1)} all-gather(bf16[2,4,128]{2,0,1:T(2,128)(2,1)S(1)} %copy.110), channel_id=1, replica_groups=mesh['grp'=4,'rep'=2,'mp'=4] {'mp'}, dimensions={1}, use_global_device_ids=true | all-gather | bytes 10240 | tf_op jit(solution)/shard_map/all_gather | solution.py:48
  87.4 66.2 %all-gather.3.cloned.1.call-done = bf16[4096,16,128]{0,2,1:T(8,128)(2,1)} async-done(((bf16[4096,16,32]{0,2,1:T(8,128)(2,1)}), bf16[4096,16,128]{0,2,1:T(8,128)(2,1)}) %all-gather.3.cloned.1.call-update) | async-done | bytes 16777232 | tf_op jit(solution)/shard_map/all_gather | solution.py:35
  153.6 8.0 %fusion = f32[4,16,128]{2,0,1:T(4,128)S(1)} fusion(bf16[4096,16,128]{0,2,1:T(8,128)(2,1)} %all-gather.3.cloned.1.call-done, bf16[4,4096]{1,0:T(4,128)(2,1)S(1)} %gather_fusion.1, pred[4]{0:T(512)(128)(4,1)S(1)} %get-tuple-element.16), kind=kOutput, calls=%fused_computation.5 | convolution fusion | flops 67125248 | bytes 16842756 | tf_op jit(solution)/shard_map/dot_general | solution.py:32
  161.6 8.1 %convolution_select_fusion = f32[4,16,128]{2,0,1:T(4,128)S(1)} fusion(f32[4,16,128]{2,0,1:T(4,128)S(1)} %fusion, bf16[16,128,4096]{2,1,0:T(8,128)(2,1)} %bitcast.76, pred[4]{0:T(512)(128)(4,1)S(1)} %get-tuple-element.15, bf16[4,4096]{1,0:T(4,128)(2,1)S(1)} %gather_fusion.1, pred[4]{0:T(512)(128)(4,1)S(1)} %get-tuple-element.16), kind=kOutput, calls=%fused_computation.13 | convolution fusion | flops 67133440 | bytes 16875528 | tf_op jit(solution)/shard_map/dot_general | solution.py:32
  169.8 0.6 copy.97
  170.5 0.6 gather_fusion.2
  171.0 0.6 gather_fusion.3
  171.6 8.9 %reduce-scatter.2.cloned.1.call-done = f32[2,16,128]{2,1,0:T(8,128)} async-done(((f32[4,16,128]{2,1,0:T(8,128)}), f32[2,16,128]{2,1,0:T(8,128)}) %reduce-scatter.2.cloned.1.call-update) | async-done | bytes 16400 | tf_op jit(solution)/shard_map/reduce_scatter | solution.py:41
  180.6 0.9 multiply_reduce_fusion
  181.4 13.2 %all_gather.13 = bf16[2,64,128]{2,0,1:T(2,128)(2,1)S(1)} all-gather(bf16[2,16,128]{2,0,1:T(2,128)(2,1)S(1)} %get-tuple-element.14), channel_id=1, replica_groups=mesh['grp'=4,'rep'=2,'mp'=4] {'mp'}, dimensions={1}, use_global_device_ids=true | all-gather | bytes 40960 | tf_op jit(solution)/shard_map/all_gather | solution.py:47
  195.2 0.7 copy.104
  195.9 4.6 %all-to-all-start.1 = ((bf16[1,2,64]{1,0,2:T(2,128)(2,1)}), bf16[1,2,64]{1,0,2:T(2,128)(2,1)S(1)}, u32[]{:S(2)}, u32[]{:S(2)}) async-start(bf16[1,2,64]{1,0,2:T(2,128)(2,1)} %copy.104), calls=%async_computation.2 | async-start | bytes 65536 | tf_op jit(solution)/shard_map/all_to_all | solution.py:80
  201.1 0.7 copy.113
  201.9 0.6 copy.102
  202.5 3.6 %all-to-all-done.1 = bf16[1,2,64]{1,0,2:T(2,128)(2,1)S(1)} async-done(((bf16[1,2,64]{1,0,2:T(2,128)(2,1)}), bf16[1,2,64]{1,0,2:T(2,128)(2,1)S(1)}, u32[]{:S(2)}, u32[]{:S(2)}) %all-to-all-start.1) | async-done | bytes 288 | tf_op jit(solution)/shard_map/all_to_all | solution.py:80
  206.1 3.3 %all-to-all-start.2 = ((bf16[1,2,64]{1,0,2:T(2,128)(2,1)}), bf16[1,2,64]{1,0,2:T(2,128)(2,1)S(1)}, u32[]{:S(2)}, u32[]{:S(2)}) async-start(bf16[1,2,64]{1,0,2:T(2,128)(2,1)} %copy.113), calls=%async_computation.3 | async-start | bytes 65536 | tf_op jit(solution)/shard_map/all_to_all | solution.py:83
  209.6 5.5 %all-to-all-done.2 = bf16[1,2,64]{1,0,2:T(2,128)(2,1)S(1)} async-done(((bf16[1,2,64]{1,0,2:T(2,128)(2,1)}), bf16[1,2,64]{1,0,2:T(2,128)(2,1)S(1)}, u32[]{:S(2)}, u32[]{:S(2)}) %all-to-all-start.2) | async-done | bytes 288 | tf_op jit(solution)/shard_map/all_to_all | solution.py:83
  215.1 3.3 %all-to-all-start = ((bf16[1,2,64,128]{3,1,0,2:T(2,128)(2,1)}), bf16[1,2,64,128]{3,1,0,2:T(2,128)(2,1)S(1)}, u32[]{:S(2)}, u32[]{:S(2)}) async-start(bf16[1,2,64,128]{3,1,0,2:T(2,128)(2,1)} %copy.102), calls=%async_computation.1 | async-start | bytes 65536 | tf_op jit(solution)/shard_map/all_to_all | solution.py:77
  218.6 5.4 %all-to-all-done = bf16[1,2,64,128]{3,1,0,2:T(2,128)(2,1)S(1)} async-done(((bf16[1,2,64,128]{3,1,0,2:T(2,128)(2,1)}), bf16[1,2,64,128]{3,1,0,2:T(2,128)(2,1)S(1)}, u32[]{:S(2)}, u32[]{:S(2)}) %all-to-all-start) | async-done | bytes 32800 | tf_op jit(solution)/shard_map/all_to_all | solution.py:77
  224.1 0.7 divide_convert_fusion
  (52 shorter events, 2.6 us)
Async XLA Ops:
  6.5 188.1 %copy-start = (bf16[2,256,8,128]{3,2,1,0:T(8,128)(2,1)S(1)}, bf16[2,256,8,128]{3,2,1,0:T(8,128)(2,1)}, u32[]{:S(2)}) copy-start(bf16[2,256,8,128]{3,2,1,0:T(8,128)(2,1)} %param.20) | copy-start | bytes 3145732
  6.5 1.6 copy-start.5
  6.5 2.3 %copy-start.1 = (s32[4]{0:T(128)S(1)}, s32[4]{0:T(128)}, u32[]{:S(2)}) copy-start(s32[4]{0:T(128)} %param.13) | copy-start | bytes 52
  6.5 3.0 %copy-start.2 = (bf16[4,4096]{1,0:T(4,128)(2,1)S(1)}, bf16[4,4096]{1,0:T(4,128)(2,1)}, u32[]{:S(2)}) copy-start(bf16[4,4096]{1,0:T(4,128)(2,1)} %param.12) | copy-start | bytes 98308
  6.5 59.4 %all-gather.5.cloned.1.call-start = ((), (), s32[]{:S(2)}) async-start(), calls=%async_computation.6 | async-start | bytes 5242880 | tf_op jit(solution)/shard_map/all_gather | solution.py:36
  7.3 146.3 %all-gather.3.cloned.1.call-start = ((), (), s32[]{:S(2)}) async-start(), calls=%async_computation.4 | async-start | bytes 20971520 | tf_op jit(solution)/shard_map/all_gather | solution.py:35
  8.0 172.5 %reduce-scatter.2.cloned.1.call-start = ((), (), s32[]{:S(2)}) async-start(), calls=%async_computation.5 | async-start | bytes 49152 | tf_op jit(solution)/shard_map/reduce_scatter | solution.py:41
  38.7 21.2 %copy-start.6 = (u32[32]{0:T(128)S(1)}, u32[32]{0:T(128)}, u32[]{:S(2)}) copy-start(u32[32]{0:T(128)} %constant.78) | copy-start | bytes 388
  38.7 22.6 %copy-start.4 = (s32[2]{0:T(128)S(1)}, s32[2]{0:T(128)}, u32[]{:S(2)}) copy-start(s32[2]{0:T(128)} %param.15) | copy-start | bytes 28
  161.6 38.8 %copy-start.3 = (bf16[2,256,8,128]{3,2,1,0:T(8,128)(2,1)S(1)}, bf16[2,256,8,128]{3,2,1,0:T(8,128)(2,1)}, u32[]{:S(2)}) copy-start(bf16[2,256,8,128]{3,2,1,0:T(8,128)(2,1)} %param.21) | copy-start | bytes 3145732
  195.9 10.2 %all-to-all-start.1 = ((bf16[1,2,64]{1,0,2:T(2,128)(2,1)}), bf16[1,2,64]{1,0,2:T(2,128)(2,1)S(1)}, u32[]{:S(2)}, u32[]{:S(2)}) async-start(bf16[1,2,64]{1,0,2:T(2,128)(2,1)} %copy.104), calls=%async_computation.2 | async-start | bytes 65536 | tf_op jit(solution)/shard_map/all_to_all | solution.py:80
  206.1 8.9 %all-to-all-start.2 = ((bf16[1,2,64]{1,0,2:T(2,128)(2,1)}), bf16[1,2,64]{1,0,2:T(2,128)(2,1)S(1)}, u32[]{:S(2)}, u32[]{:S(2)}) async-start(bf16[1,2,64]{1,0,2:T(2,128)(2,1)} %copy.113), calls=%async_computation.3 | async-start | bytes 65536 | tf_op jit(solution)/shard_map/all_to_all | solution.py:83
  215.1 8.9 %all-to-all-start = ((bf16[1,2,64,128]{3,1,0,2:T(2,128)(2,1)}), bf16[1,2,64,128]{3,1,0,2:T(2,128)(2,1)S(1)}, u32[]{:S(2)}, u32[]{:S(2)}) async-start(bf16[1,2,64,128]{3,1,0,2:T(2,128)(2,1)} %copy.102), calls=%async_computation.1 | async-start | bytes 65536 | tf_op jit(solution)/shard_map/all_to_all | solution.py:77
Sparse Core Ops, SparseCore 0:
  8.9 37.1 all-gather.4
  47.7 105.8 all-gather.2
  170.6 9.9 reduce-scatter.1
where the time goes:
time: 233 us; the launch traced here: 231 us
  waiting for transfers between devices  91 us (39%)
  local copies, waits for them, and re-layouts  56.2 us (24%)
  blocking collectives  31.1 us (13%)
  matrix products  25.1 us (11%)
  between operations  13.9 us (6%)
  starting transfers between devices  11.2 us (5%)
  other arithmetic  2.81 us (1%)
    all_gather x1, waiting for transfers between devices, local(): fresh_queries = project(lax.all_gather(fresh_q, 'grp', axis=2, tiled=True))  66.2 us
    dot_general x2, local copies, waits for them, and re-layouts, project(): jnp.dot(slot_inputs, flat_weight, preferred_element_type=jnp.float32)  27.7 us
    dot_general x4, matrix products, project(): jnp.dot(slot_inputs, flat_weight, preferred_element_type=jnp.float32)  24.4 us
    unnamed x17, local copies, waits for them, and re-layouts  22.7 us
    all_gather x1, blocking collectives, local(): lax.all_gather(my_queries, 'mp', axis=1, tiled=True)  13.2 us
    all_gather x1, blocking collectives, local(): lax.all_gather(my_slots, 'mp', axis=1, tiled=True)  12.6 us
    reduce_scatter x1, waiting for transfers between devices, local(): lax.psum_scatter(query_terms, 'rep', scatter_dimension=0, tiled=True)  8.92 us
    all_to_all x1, waiting for transfers between devices, local(): lax.all_to_all(local_sum[None].astype(jnp.bfloat16), 'mp', split_axis=2,...  5.46 us
  transfers between devices with their start and end apart: 6, of which 5 were waited for; matrix products, arithmetic and copies ran while one was open for 28% of the time, Pallas kernels for 0%

commit v1 on v0

v1 whole, which is shorter than its diff:
```python
import functools
import math

import jax
import jax.numpy as jnp
from jax import lax
from jax.sharding import PartitionSpec as P

AXES = ("grp", "rep", "mp")


def slot_order(inputs, stale_rows, row_order):
    lanes = 128
    flags = jnp.broadcast_to(stale_rows.astype(inputs.dtype)[:, None], (inputs.shape[0], lanes))
    rows = jnp.concatenate([inputs, flags], axis=1)
    slots = jnp.arange(inputs.shape[0], dtype=row_order.dtype)
    moved = 0
    for i in range(inputs.shape[0]):
        moved = moved + jnp.where((slots == row_order[i])[:, None], rows[i][None], 0)
    return moved


def plain(
    sizes, inputs, stale_rows, row_order, lengths, old_q, old_kv, fresh_q, fresh_kv, key_cache, value_cache
):
    n_grp, n_rep, n_mp = sizes
    part_width = inputs.shape[1]
    heads_here = old_q.shape[1]
    head_size = old_q.shape[2]
    slice_here = fresh_q.shape[2]
    slots_here = heads_here + old_kv.shape[1]
    gathered = lax.all_gather(slot_order(inputs, stale_rows, row_order), "grp", axis=0, tiled=True)
    rows_all = gathered.shape[0]
    features = gathered[:, :part_width]
    stale = gathered[:, part_width] == 1
    first = lax.axis_index("grp") * slice_here

    def project(q, kv):
        parts = [jnp.einsum("bf,fhd->bhd", features, w, preferred_element_type=jnp.float32) for w in (q, kv)]
        return jnp.concatenate(parts, axis=1)

    cut = functools.partial(lax.dynamic_slice_in_dim, start_index=first, slice_size=slice_here, axis=2)
    terms = jnp.where(stale[:, None, None], project(cut(old_q), cut(old_kv)), project(fresh_q, fresh_kv))
    rows_here = rows_all // (n_grp * n_rep)
    terms = terms.reshape(n_grp * n_rep, 1, rows_here * slots_here * slice_here)
    terms = jnp.broadcast_to(terms, (n_grp * n_rep, n_mp, terms.shape[2]))
    terms = terms.reshape(n_grp * n_rep * n_mp, 1, terms.shape[2])
    held = lax.all_to_all(terms, AXES, 0, 0, tiled=True)
    held = held.reshape(n_grp, n_rep, n_mp, rows_here, slots_here, slice_here)
    held = jnp.sum(held, axis=1).astype(jnp.bfloat16)
    held = jnp.transpose(held, (2, 1, 3, 0, 4)).reshape(rows_here, n_mp, slots_here, head_size)
    queries = held[:, :, :heads_here].reshape(rows_here, n_mp * heads_here, head_size)
    slots = held[:, :, heads_here:].reshape(rows_here, -1, head_size)
    kv_heads = slots.shape[1] // 2
    head_count = queries.shape[1]
    per_group = head_count // kv_heads
    scale = 1.0 / math.sqrt(head_size)
    grouped = queries.reshape(rows_here, kv_heads, per_group, head_size)
    scores = jnp.einsum("bkgd,blkd->bkgl", grouped, key_cache, preferred_element_type=jnp.float32) * scale
    positions_here = key_cache.shape[1]
    positions = lax.axis_index("mp") * positions_here + jnp.arange(positions_here, dtype=jnp.int32)
    allowed = (positions[None, :] < lengths[:, None])[:, None, None, :]
    new_keys = slots[:, :kv_heads, None].astype(jnp.float32)
    new_values = slots[:, kv_heads:, None].astype(jnp.float32)
    new_score = jnp.sum(grouped.astype(jnp.float32) * new_keys, axis=-1) * scale
    new_score = jnp.where(lax.axis_index("mp") == 0, new_score, -1e30)
    top = jnp.maximum(jnp.max(jnp.where(allowed, scores, -1e30), axis=-1), new_score)
    probable = jnp.where(allowed, jnp.exp(scores - top[..., None]), 0.0)
    new_weight = jnp.where(lax.axis_index("mp") == 0, jnp.exp(new_score - top), 0.0)
    total = jnp.sum(probable, axis=-1) + new_weight
    out = jnp.einsum("bkgl,blkd->bkgd", probable.astype(jnp.bfloat16), value_cache, preferred_element_type=jnp.float32)
    out = out + new_weight[..., None] * new_values
    flat = (rows_here, head_count)
    part = jnp.concatenate(
        [out.reshape(*flat, head_size), top.reshape(*flat, 1), total.reshape(*flat, 1)], axis=2
    )
    part = lax.all_to_all(part[None], "mp", split_axis=2, concat_axis=0, tiled=True)
    outs, tops, totals = part[..., :head_size], part[..., head_size], part[..., head_size + 1]
    weights = jnp.exp(tops - jnp.max(tops, axis=0)[None])
    numerator = jnp.sum(outs * weights[..., None], axis=0)
    return (numerator / jnp.sum(totals * weights, axis=0)[..., None]).astype(jnp.bfloat16)


def solution(mesh):
    sizes = tuple(mesh.shape[a] for a in AXES)
    return jax.shard_map(
        functools.partial(plain, sizes),
        mesh=mesh,
        in_specs=(
            P("grp", "rep"),
            P("grp"),
            P("grp"),
            P(("grp", "rep")),
            P("rep", "mp", None),
            P("rep", "mp", None),
            P("rep", "mp", "grp"),
            P("rep", "mp", "grp"),
            P(("grp", "rep"), "mp", None, None),
            P(("grp", "rep"), "mp", None, None),
        ),
        out_specs=P(("grp", "rep"), "mp", None),
        check_vma=False,
    )
```

time: 233 us -> 63 us (0.27)
  waiting for transfers between devices: 91 us -> 8 us
  local copies, waits for them, and re-layouts: 56.2 us -> 19.1 us
  matrix products: 25.1 us -> 7.41 us
  blocking collectives: 31.1 us -> 15.4 us
  between operations: 13.9 us -> 0.31 us
  starting transfers between devices: 11.2 us -> 6.19 us
  other arithmetic: 2.81 us -> 6.09 us
    all_gather x2 -> x0, waiting for transfers between devices: 66.2 us -> none  [the longest x1 66.2 us: local(): fresh_queries = project(lax.all_gather(fresh_q, 'grp', axis=2, tiled=True))]
    dot_general x2 -> x0, local copies, waits for them, and re-layouts: 27.7 us -> none  [project(): jnp.dot(slot_inputs, flat_weight, preferred_element_type=jnp.float32)]
    unnamed x17 -> x13, local copies, waits for them, and re-layouts: 22.7 us -> 1.58 us
    all_gather x2 -> x1, blocking collectives: 25.7 us -> 6.56 us  [plain(): lax.all_gather(slot_order(inputs, stale_rows, row_order), 'grp', axis=0,...]
    dot_general x6, matrix products: 25.1 us -> 7.41 us  [the longest x4 6.65 us: project(): jnp.einsum('bf,fhd->bhd', features, w, preferred_element_type=jnp.float32)]
    dynamic_slice x0 -> x2, local copies, waits for them, and re-layouts: none -> 12.6 us  [the longest x1 10 us: plain(): cut(old_q)]
    reduce_scatter x1 -> x0, waiting for transfers between devices: 8.92 us -> none  [local(): lax.psum_scatter(query_terms, 'rep', scatter_dimension=0, tiled=True)]
    all_to_all x0 -> x1, blocking collectives: none -> 8.89 us  [plain(): lax.all_to_all(part[None], 'mp', split_axis=2, concat_axis=0, tiled=True)]
  transfers between devices with their start and end apart: 6 -> 1, of which waited for: 5 -> 1; matrix products, arithmetic and copies ran while one was open for 28% -> 0% of each run, Pallas kernels for 0% -> 0%
where the time goes in v1:
time: 63 us; the launch traced here: 62.5 us
  local copies, waits for them, and re-layouts  19.1 us (30%)
  blocking collectives  15.4 us (24%)
  waiting for transfers between devices  8 us (13%)
  matrix products  7.41 us (12%)
  starting transfers between devices  6.19 us (10%)
  other arithmetic  6.09 us (10%)
    dynamic_slice x1, local copies, waits for them, and re-layouts, plain(): cut(old_q)  10 us
    all_to_all x1, blocking collectives, plain(): lax.all_to_all(part[None], 'mp', split_axis=2, concat_axis=0, tiled=True)  8.89 us
    all_to_all x1, waiting for transfers between devices, plain(): held = lax.all_to_all(terms, AXES, 0, 0, tiled=True)  8 us
    dot_general x4, matrix products, project(): jnp.einsum('bf,fhd->bhd', features, w, preferred_element_type=jnp.float32)  6.65 us
    all_gather x1, blocking collectives, plain(): lax.all_gather(slot_order(inputs, stale_rows, row_order), 'grp', axis=0,...  6.56 us
    all_to_all x1, starting transfers between devices, plain(): held = lax.all_to_all(terms, AXES, 0, 0, tiled=True)  6.19 us
    dynamic_slice x1, local copies, waits for them, and re-layouts, plain(): cut(old_kv)  2.55 us
    eq x2, other arithmetic, slot_order(): slots == row_order[i]  2.54 us
  transfers between devices with their start and end apart: 1, of which 1 were waited for; matrix products, arithmetic and copies ran while one was open for 0% of the time, Pallas kernels for 0%

profile of v1, /device:TPU:0, one launch (start us, length us, event | category | flops | bytes accessed | tf_op | source)
XLA Modules:
  0.0 62.5 jit_solution(11283180343242958985)
XLA Ops:
  0.0 1.5 %fusion.29 = (s32[1]{0:T(128)}, s32[1]{0:T(128)}, s32[1]{0:T(128)}, s32[1]{0:T(128)}) fusion(s32[4]{0:T(128)} %param.12), kind=kLoop, calls=%fused_computation.64 | loop fusion | bytes 32 | tf_op jit(solution)/shard_map/slice | solution.py:19
  1.5 0.7 %convert_element_type.33 = bf16[4]{0:T(256)(128)(2,1)S(1)} convert(s32[4]{0:T(128)} %param.11) | non-fusion elementwise | flops 4 | bytes 24 | tf_op jit(solution)/shard_map/convert_element_type | solution.py:14
  2.1 1.2 %iota_compare_fusion = (pred[4]{0:T(512)(128)(4,1)S(1)}, pred[4]{0:T(512)(128)(4,1)S(1)}) fusion(s32[]{:T(128)} %bitcast.3, s32[]{:T(128)} %bitcast.2), kind=kLoop, calls=%fused_computation.57 | loop fusion | flops 8 | bytes 16 | tf_op jit(solution)/shard_map/eq | solution.py:19
  3.3 1.3 %iota_compare_fusion.2 = (pred[4]{0:T(512)(128)(4,1)S(1)}, pred[4]{0:T(512)(128)(4,1)S(1)}) fusion(s32[]{:T(128)} %bitcast.1, s32[]{:T(128)} %bitcast), kind=kLoop, calls=%fused_computation.59 | loop fusion | flops 8 | bytes 16 | tf_op jit(solution)/shard_map/eq | solution.py:19
  4.8 1.1 %fusion.21 = (bf16[4224]{0:T(1024)(128)(2,1)S(1)}, bf16[4224]{0:T(1024)(128)(2,1)S(1)}, bf16[4224]{0:T(1024)(128)(2,1)S(1)}, bf16[4224]{0:T(1024)(128)(2,1)S(1)}) fusion(bf16[4,128]{1,0:T(4,128)(2,1)S(1)} %broadcast_in_dim.127, bf16[4,4096]{1,0:T(4,128)(2,1)} %param.10), kind=kLoop, calls=%fused_computation.39 | loop fusion | flops 67584 | bytes 67584 | tf_op jit(solution)/shard_map/slice | solution.py:19
  6.0 6.6 %all-gather = bf16[4,4,4224]{2,1,0:T(4,128)(2,1)S(1)} all-gather(bf16[1,4,4224]{2,1,0:T(4,128)(2,1)S(1)} %add_bitcast_fusion), channel_id=1, replica_groups=mesh['grp'=4,'rep'=2,'mp'=4] {'grp'}, dimensions={0}, use_global_device_ids=true | all-gather | bytes 168960 | tf_op jit(solution)/shard_map/all_gather | solution.py:32
  12.6 0.1 compare_reduce_fusion
  12.7 10.0 %constant_dynamic-slice_fusion.1 = bf16[4096,16,32]{2,1,0:T(8,128)(2,1)S(1)} fusion(bf16[4096,16,128]{2,1,0:T(8,128)(2,1)} %param.14, s32[]{:T(128)S(6)} %select_n.92), kind=kLoop, calls=%fused_computation.56 | loop fusion | bytes 8388612 | tf_op jit(solution)/shard_map/dynamic_slice | solution.py:43
  22.8 2.4 %fusion = f32[16,16,32]{2,0,1:T(8,128)S(1)} fusion(bf16[4096,16,32]{2,1,0:T(8,128)(2,1)S(1)} %constant_dynamic-slice_fusion.1, bf16[16,4224]{1,0:T(8,128)(2,1)S(1)} %reshape.178), kind=kOutput, calls=%fused_computation | convolution fusion | flops 67108864 | bytes 16941056 | tf_op jit(solution)/shard_map/bf,fhd->bhd/dot_general | solution.py:39
  25.2 2.6 %constant_dynamic-slice_fusion = bf16[4096,4,32]{2,1,0:T(4,128)(2,1)S(1)} fusion(bf16[4096,4,128]{2,1,0:T(4,128)(2,1)S(1)} %copy-done.1, s32[]{:T(128)S(6)} %select_n.92), kind=kLoop, calls=%fused_computation.55 | loop fusion | bytes 2097156 | tf_op jit(solution)/shard_map/dynamic_slice | solution.py:43
  27.7 0.7 %fusion.2 = f32[16,4,32]{2,0,1:T(8,128)S(1)} fusion(bf16[4096,4,32]{2,1,0:T(4,128)(2,1)S(1)} %constant_dynamic-slice_fusion, bf16[16,4224]{1,0:T(8,128)(2,1)S(1)} %reshape.178), kind=kOutput, calls=%fused_computation.2 | convolution fusion | flops 16777216 | bytes 4333568 | tf_op jit(solution)/shard_map/bf,fhd->bhd/dot_general | solution.py:39
  28.4 1.5 %copy-done.2 = bf16[4096,16,32]{0,2,1:T(8,128)(2,1)S(1)} copy-done((bf16[4096,16,32]{0,2,1:T(8,128)(2,1)S(1)}, bf16[4096,16,32]{0,2,1:T(8,128)(2,1)}, u32[]{:S(2)}) %copy-start.2) | copy-done | bytes 4194328
  29.9 2.8 %fusion.16 = f32[16,16,32]{2,0,1:T(8,128)S(1)} fusion(bf16[4096,16,32]{0,2,1:T(8,128)(2,1)S(1)} %copy-done.2, bf16[16,4224]{1,0:T(8,128)(2,1)S(1)} %reshape.178), kind=kOutput, calls=%fused_computation.29 | convolution fusion | flops 67108864 | bytes 4358144 | tf_op jit(solution)/shard_map/bf,fhd->bhd/dot_general | solution.py:39
  32.7 0.8 %fusion.15 = f32[16,4,32]{2,0,1:T(8,128)S(1)} fusion(bf16[4096,4,32]{0,2,1:T(8,128)(2,1)S(1)} %copy-done.3, bf16[16,4224]{1,0:T(8,128)(2,1)S(1)} %reshape.178), kind=kOutput, calls=%fused_computation.28 | convolution fusion | flops 16777216 | bytes 1187840 | tf_op jit(solution)/shard_map/bf,fhd->bhd/dot_general | solution.py:39
  33.8 0.8 %reshape.172 = f32[32,1,1280]{2,1,0:T(1,128)} reshape(f32[8,4,1280]{2,1,0:T(4,128)S(1)} %broadcast_in_dim.141) | data formatting | bytes 327680 | tf_op jit(solution)/shard_map/reshape | solution.py:47
  34.7 6.2 %all-to-all-start = ((f32[32,1,1280]{2,1,0:T(1,128)}), f32[32,1,1280]{2,1,0:T(1,128)S(1)}, u32[]{:S(2)}, u32[]{:S(2)}) async-start(f32[32,1,1280]{2,1,0:T(1,128)} %reshape.172), calls=%async_computation | async-start | bytes 327680 | tf_op jit(solution)/shard_map/all_to_all | solution.py:48
  41.0 8.0 %all-to-all-done = f32[32,1,1280]{2,1,0:T(1,128)S(1)} async-done(((f32[32,1,1280]{2,1,0:T(1,128)}), f32[32,1,1280]{2,1,0:T(1,128)S(1)}, u32[]{:S(2)}, u32[]{:S(2)}) %all-to-all-start) | async-done | bytes 163872 | tf_op jit(solution)/shard_map/all_to_all | solution.py:48
  49.0 0.4 reduce.7
  49.4 0.3 reshape.173
  49.8 0.1 copy.85
  49.9 0.1 reshape.174
  50.1 0.1 fusion.11
  50.5 0.5 select_reduce_fusion
  51.1 0.2 fusion.8
  51.3 0.3 fusion.4
  51.7 0.1 copy.94
  51.8 0.1 copy.95
  52.0 0.1 maximum_bitcast_fusion
  52.1 8.9 %all_to_all.23 = f32[1,2,64,130]{3,1,0,2:T(2,128)S(1)} all-to-all(f32[1,2,64,130]{3,1,0,2:T(2,128)S(1)} %maximum_bitcast_fusion), channel_id=1, replica_groups=mesh['grp'=4,'rep'=2,'mp'=4] {'mp'}, dimensions={2} | all-to-all | bytes 133120 | tf_op jit(solution)/shard_map/all_to_all | solution.py:77
  61.0 0.4 copy.97
  61.4 0.4 fusion.7
  61.8 0.7 %copy.102 = bf16[2,16,128]{2,1,0:T(8,128)(2,1)} copy(bf16[2,16,128]{1,2,0:T(8,128)(2,1)S(1)} %divide_convert_fusion) | data formatting | bytes 16384 | tf_op jit(solution)/shard_map/convert_element_type | solution.py:81
  (40 shorter events, 1.3 us)
Async XLA Ops:
  0.0 50.5 %copy-start = (bf16[2,256,8,128]{3,2,1,0:T(8,128)(2,1)S(1)}, bf16[2,256,8,128]{3,2,1,0:T(8,128)(2,1)}, u32[]{:S(2)}) copy-start(bf16[2,256,8,128]{3,2,1,0:T(8,128)(2,1)} %param.18) | copy-start | bytes 3145732
  22.7 2.4 %copy-start.1 = (bf16[4096,4,128]{2,1,0:T(4,128)(2,1)S(1)}, bf16[4096,4,128]{2,1,0:T(4,128)(2,1)}, u32[]{:S(2)}) copy-start(bf16[4096,4,128]{2,1,0:T(4,128)(2,1)} %param.15) | copy-start | bytes 12582916
  27.7 2.2 %copy-start.2 = (bf16[4096,16,32]{0,2,1:T(8,128)(2,1)S(1)}, bf16[4096,16,32]{0,2,1:T(8,128)(2,1)}, u32[]{:S(2)}) copy-start(bf16[4096,16,32]{0,2,1:T(8,128)(2,1)} %param.16) | copy-start | bytes 12582916
  27.7 5.0 %copy-start.3 = (bf16[4096,4,32]{0,2,1:T(8,128)(2,1)S(1)}, bf16[4096,4,32]{0,2,1:T(8,128)(2,1)}, u32[]{:S(2)}) copy-start(bf16[4096,4,32]{0,2,1:T(8,128)(2,1)} %param.17) | copy-start | bytes 3145732
  29.9 11.0 %copy-start.5 = (s32[2]{0:T(128)S(1)}, s32[2]{0:T(128)}, u32[]{:S(2)}) copy-start(s32[2]{0:T(128)} %param.13) | copy-start | bytes 28
  32.7 18.5 %copy-start.4 = (bf16[2,256,8,128]{3,2,1,0:T(8,128)(2,1)S(1)}, bf16[2,256,8,128]{3,2,1,0:T(8,128)(2,1)}, u32[]{:S(2)}) copy-start(bf16[2,256,8,128]{3,2,1,0:T(8,128)(2,1)} %param.19) | copy-start | bytes 3145732
  34.7 14.3 %all-to-all-start = ((f32[32,1,1280]{2,1,0:T(1,128)}), f32[32,1,1280]{2,1,0:T(1,128)S(1)}, u32[]{:S(2)}, u32[]{:S(2)}) async-start(f32[32,1,1280]{2,1,0:T(1,128)} %reshape.172), calls=%async_computation | async-start | bytes 327680 | tf_op jit(solution)/shard_map/all_to_all | solution.py:48

commit v2 on v1

--- a/solution.py
+++ b/solution.py
@@ -4,6 +4,8 @@
 import jax
 import jax.numpy as jnp
 from jax import lax
+from jax.experimental import pallas as pl
+from jax.experimental.pallas import tpu as pltpu
 from jax.sharding import PartitionSpec as P
 
 AXES = ("grp", "rep", "mp")
@@ -81,10 +83,333 @@
     return (numerator / jnp.sum(totals * weights, axis=0)[..., None]).astype(jnp.bfloat16)
 
 
+LANES = 128
+SUBLANES = 8
+HBM = pltpu.MemorySpace.HBM
+VMEM = pltpu.MemorySpace.VMEM
+SMEM = pltpu.MemorySpace.SMEM
+ROOMY = 67_043_328
+START_BYTES = 32 << 20
+
+
+def whole_block(space):
+    return pl.BlockSpec(memory_space=space)
+
+
+def order_kernel(order_in, stale_in, rows_in, moved, order, stale, rows, sems):
+    pairs = ((order_in, order), (stale_in, stale), (rows_in, rows))
+    copies = [pltpu.make_async_copy(a, b, sems.at[n]) for n, (a, b) in enumerate(pairs)]
+    for copy in copies:
+        copy.start()
+    for copy in copies:
+        copy.wait()
+    count, width = rows.shape
+    where_row = lax.broadcasted_iota(jnp.int32, (count, 1), 0)
+    total = jnp.zeros((count, width), jnp.float32)
+    flags = jnp.zeros((count, LANES), jnp.float32)
+    for i in range(count):
+        here = where_row == order[i]
+        total = jnp.where(here, rows[i : i + 1, :].astype(jnp.float32), total)
+        flags = jnp.where(here, stale[i].astype(jnp.float32), flags)
+    moved[:, :width] = total.astype(moved.dtype)
+    moved[:, width:] = flags.astype(moved.dtype)
+
+
+def load_kernel(old_q, near, sem):
+    copy = pltpu.make_async_copy(old_q.at[:, lax.axis_index("grp")], near, sem)
+    copy.start()
+    copy.wait()
+
+
+def project_kernel(n_rep, n_mp, *refs):
+    rows_in = refs[:-7]
+    old_q, old_kv, fresh_q, fresh_kv, out, features, staged = refs[-7:]
+    n_grp = len(rows_in)
+    mine = lax.axis_index("grp")
+    group_rows, width = rows_in[0].shape
+    rows = group_rows * n_grp
+    part_width = width - LANES
+    per_row = old_q.shape[0] // part_width
+    for k, part in enumerate(rows_in):
+        features[k * group_rows : (k + 1) * group_rows, :] = part[...]
+    chunks = part_width // LANES
+    stacked = jnp.concatenate([features[:, c * LANES : (c + 1) * LANES] for c in range(chunks)], axis=0)
+    spread_width = LANES * per_row
+    source = lax.broadcasted_iota(jnp.int32, (LANES, spread_width), 0)
+    target = lax.broadcasted_iota(jnp.int32, (LANES, spread_width), 1)
+    spread = jnp.where(target // per_row == source, 1.0, 0.0).astype(jnp.bfloat16)
+    wide = jnp.dot(stacked, spread, preferred_element_type=jnp.float32).astype(jnp.bfloat16)
+    lane = lax.broadcasted_iota(jnp.int32, (1, spread_width), 1) % per_row
+    picks = [jnp.where(lane == h, 1.0, 0.0).astype(jnp.bfloat16) for h in range(per_row)]
+    old = jnp.zeros((per_row * rows, 2 * LANES), jnp.float32)
+    for c in range(chunks):
+        piece = wide[c * rows : (c + 1) * rows]
+        left = jnp.concatenate([piece * pick for pick in picks], axis=0)
+        span = slice(c * spread_width, (c + 1) * spread_width)
+        right = jnp.concatenate([old_q[span, :], old_kv[span, :]], axis=1)
+        old = old + jnp.dot(left, right, preferred_element_type=jnp.float32)
+    values = features[:, :part_width]
+    across = (((1,), (1,)), ((), ()))
+    new_q = lax.dot_general(values, fresh_q[...], across, preferred_element_type=jnp.float32)
+    new_kv = lax.dot_general(values, fresh_kv[...], across, preferred_element_type=jnp.float32)
+    stale = features[:, part_width : part_width + 1].astype(jnp.float32) == 1.0
+    for j in range(per_row):
+        span = slice(j * LANES, (j + 1) * LANES)
+        staged[j * rows : (j + 1) * rows, :] = jnp.where(stale, old[j * rows : (j + 1) * rows, :LANES], new_q[:, span])
+    kept = old[:rows, LANES:]
+    for h in range(1, per_row):
+        kept = jnp.where(mine == h, old[h * rows : (h + 1) * rows, LANES:], kept)
+    staged[per_row * rows :, :] = jnp.where(stale, kept, new_kv)
+    parts = per_row + 1
+    rows_here = group_rows // n_rep
+    for k in range(n_grp):
+        group = jnp.bitwise_xor(mine, k)
+        for r in range(n_rep):
+            for i in range(rows_here):
+                row = k * group_rows + r * rows_here + i
+                block = staged[pl.ds(row, parts, stride=rows), :]
+                for m in range(n_mp):
+                    first = (m * rows_here + i) * parts
+                    out[group * n_rep + r, first : first + parts, :] = block
+
+
+def attend_kernel(sizes, scale, order, stale, lengths, held, keys, values, *refs):
+    n_grp, n_rep, n_mp = sizes
+    outs = refs[:n_mp]
+    summed, turned, queries, slots, packed = refs[n_mp:]
+    rows_here, places, head_size = keys.shape
+    slots_here = n_grp
+    heads_here = queries.shape[0] // (rows_here * n_mp)
+    head_count = heads_here * n_mp
+    kv_heads = slots_here * n_mp // 2
+    per_group = head_count // kv_heads
+    shares = heads_here // n_grp
+    parts = shares + 1
+    block = held.shape[1]
+    step = head_size // n_grp
+    mp = lax.axis_index("mp")
+    rep = lax.axis_index("rep")
+    sums = []
+    for g in range(n_grp):
+        total = held[g * n_rep]
+        for r in range(1, n_rep):
+            total = total + held[g * n_rep + r]
+        sums.append(total)
+        summed[g * block : (g + 1) * block, :] = total
+    lane = lax.broadcasted_iota(jnp.int32, (1, head_size), 1) // step
+    for h in range(n_grp):
+        total = sums[h]
+        for g in range(n_grp):
+            if g != h:
+                total = jnp.where(lane == g, pltpu.roll(sums[g], (step * (g - h)) % head_size, 1), total)
+        turned[h * block : (h + 1) * block, :] = total
+    lanes = lax.broadcasted_iota(jnp.int32, (SUBLANES, places), 1)
+    stats_lane = lax.broadcasted_iota(jnp.int32, (1, LANES), 1) // (LANES // (2 * rows_here))
+    stats = [jnp.zeros((per_group, LANES), jnp.float32) for _ in range(kv_heads)]
+    for i in range(rows_here):
+        flag = jnp.int32(0)
+        for n in range(order.shape[0]):
+            flag = jnp.where(order[n] == rep * rows_here + i, stale[n], flag)
+
+        @pl.when(flag == 1)
+        def _():
+            for m in range(n_mp):
+                base = (m * rows_here + i) * parts
+                for g in range(n_grp):
+                    first = i * head_count + m * heads_here + g * shares
+                    queries[first : first + shares, :] = summed[g * block + base : g * block + base + shares, :]
+                first = i * n_mp * slots_here + m * slots_here
+                slots[first : first + slots_here, :] = summed[pl.ds(base + shares, slots_here, stride=block), :]
+
+        @pl.when(flag != 1)
+        def _():
+            for m in range(n_mp):
+                base = (m * rows_here + i) * parts
+                for j in range(shares):
+                    first = i * head_count + m * heads_here + j * n_grp
+                    queries[first : first + n_grp, :] = turned[pl.ds(base + j, n_grp, stride=block), :]
+                first = i * n_mp * slots_here + m * slots_here
+                slots[first : first + slots_here, :] = turned[pl.ds(base + shares, slots_here, stride=block), :]
+
+        query = queries[i * head_count : (i + 1) * head_count, :].astype(jnp.bfloat16)
+        fresh = slots[i * 2 * kv_heads : (i + 1) * 2 * kv_heads, :].astype(jnp.bfloat16).astype(jnp.float32)
+        scores = lax.dot_general(query, keys[i], (((1,), (1,)), ((), ())), preferred_element_type=jnp.float32) * scale
+        position = mp * (places // kv_heads) + lanes // kv_heads
+        valid = position < lengths[i]
+        weights, tops, totals, added = [], [], [], []
+        for b in range(kv_heads):
+            span = slice(b * per_group, (b + 1) * per_group)
+            allowed = valid & (lanes % kv_heads == b)
+            mine = jnp.sum(query[span].astype(jnp.float32) * fresh[b : b + 1], axis=1, keepdims=True) * scale
+            mine = jnp.where(mp == 0, mine, -1e30)
+            top = jnp.max(jnp.where(allowed, scores[span], -1e30), axis=1, keepdims=True)
+            top = jnp.maximum(top, mine)
+            probable = jnp.where(allowed, jnp.exp(scores[span] - top), 0.0)
+            own = jnp.where(mp == 0, jnp.exp(mine - top), 0.0)
+            total = jnp.sum(probable, axis=1, keepdims=True) + own
+            weights.append(probable)
+            added.append(own * fresh[kv_heads + b : kv_heads + b + 1])
+            stats[b] = jnp.where(stats_lane == 2 * i, top, stats[b])
+            stats[b] = jnp.where(stats_lane == 2 * i + 1, total, stats[b])
+        weight = jnp.concatenate(weights, axis=0).astype(jnp.bfloat16)
+        out = jnp.dot(weight, values[i], preferred_element_type=jnp.float32) + jnp.concatenate(added, axis=0)
+        for m in range(n_mp):
+            packed[m, i * heads_here : (i + 1) * heads_here, :] = out[m * heads_here : (m + 1) * heads_here]
+    for m in range(n_mp):
+        here = jnp.concatenate(stats[m * heads_here // per_group : (m + 1) * heads_here // per_group], axis=0)
+        packed[m, rows_here * heads_here :, :] = here
+    for k, ref in enumerate(outs):
+        ref[...] = packed[jnp.bitwise_xor(mp, k)]
+
+
+def join_kernel(*refs):
+    parts, out = refs[:-1], refs[-1]
+    rows_here, heads_here, head_size = out.shape
+    step = LANES // (2 * rows_here)
+    stats = rows_here * heads_here
+    for i in range(rows_here):
+        tops = [p[stats:, 2 * i * step : 2 * i * step + 1] for p in parts]
+        sums = [p[stats:, (2 * i + 1) * step : (2 * i + 1) * step + 1] for p in parts]
+        joined = functools.reduce(jnp.maximum, tops)
+        scales = [jnp.exp(top - joined) for top in tops]
+        numerator = sum(p[i * heads_here : (i + 1) * heads_here, :] * s for p, s in zip(parts, scales))
+        divisor = sum(n * s for n, s in zip(sums, scales))
+        out[i] = (numerator / divisor).astype(out.dtype)
+
+
+def exchanged(value, axis, count):
+    return [value] + [lax.ppermute(value, axis, [(i, i ^ k) for i in range(count)]) for k in range(1, count)]
+
+
+def close(
+    sizes, inputs, stale_rows, row_order, lengths, old_q, old_kv, fresh_q, fresh_kv, key_cache, value_cache
+):
+    n_grp, n_rep, n_mp = sizes
+    group_rows, part_width = inputs.shape
+    heads_here = old_q.shape[1]
+    head_size = old_q.shape[2]
+    slice_here = fresh_q.shape[2]
+    rows = group_rows * n_grp
+    rows_here, positions_here, kv_heads, _ = key_cache.shape
+    shares = heads_here // n_grp
+    parts = shares + 1
+    bf16 = functools.partial(jax.ShapeDtypeStruct, dtype=jnp.bfloat16)
+    f32 = functools.partial(jax.ShapeDtypeStruct, dtype=jnp.float32)
+    moved = pl.pallas_call(
+        order_kernel,
+        out_shape=bf16((group_rows, part_width + LANES)),
+        in_specs=[whole_block(HBM)] * 3,
+        out_specs=whole_block(VMEM),
+        scratch_shapes=[
+            pltpu.SMEM((group_rows,), jnp.int32),
+            pltpu.SMEM((group_rows,), jnp.int32),
+            pltpu.VMEM((group_rows, part_width), jnp.bfloat16),
+            pltpu.SemaphoreType.DMA((3,)),
+        ],
+        compiler_params=pltpu.CompilerParams(vmem_limit_bytes=ROOMY),
+        cost_estimate=pl.CostEstimate(flops=0, bytes_accessed=START_BYTES, transcendentals=0),
+        name="order",
+    )(row_order, stale_rows, inputs)
+    gathered = exchanged(moved, "grp", n_grp)
+    share = bf16((part_width, shares, head_size))
+    near_q = pl.pallas_call(
+        load_kernel,
+        out_shape=share,
+        in_specs=[whole_block(HBM)],
+        out_specs=whole_block(pl.ANY),
+        scratch_shapes=[pltpu.SemaphoreType.DMA],
+        compiler_params=pltpu.CompilerParams(vmem_limit_bytes=40 << 20),
+        cost_estimate=pl.CostEstimate(flops=0, bytes_accessed=4 * math.prod(share.shape), transcendentals=0),
+        name="load",
+    )(old_q.reshape(part_width, n_grp, shares, head_size))
+    near = (
+        old_kv.reshape(part_width * n_grp, head_size),
+        jnp.transpose(fresh_q, (1, 2, 0)).reshape(heads_here * slice_here, part_width),
+        jnp.transpose(fresh_kv, (1, 2, 0)).reshape(n_grp * slice_here, part_width),
+    )
+    block = n_mp * rows_here * parts
+    terms = pl.pallas_call(
+        functools.partial(project_kernel, n_rep, n_mp),
+        out_shape=f32((n_grp * n_rep, block, head_size)),
+        in_specs=[whole_block(VMEM)] * (n_grp + 4),
+        out_specs=whole_block(VMEM),
+        scratch_shapes=[
+            pltpu.VMEM((rows, part_width + LANES), jnp.bfloat16),
+            pltpu.VMEM((rows * parts, LANES), jnp.float32),
+        ],
+        compiler_params=pltpu.CompilerParams(vmem_limit_bytes=24 << 20),
+        name="project",
+    )(*gathered, near_q.reshape(part_width * shares, head_size), *near)
+    devices = n_grp * n_rep * n_mp
+    held = lax.all_to_all(terms.reshape(devices, 1, rows_here * parts * head_size), AXES, 0, 0, tiled=True)
+    held = held.reshape(n_grp * n_rep, block, head_size)
+    places = positions_here * kv_heads
+    packed_rows = (rows_here + 1) * heads_here
+    partial_out = pl.pallas_call(
+        functools.partial(attend_kernel, sizes, 1.0 / math.sqrt(head_size)),
+        out_shape=[f32((packed_rows, LANES))] * n_mp,
+        in_specs=[whole_block(SMEM)] * 3 + [whole_block(VMEM)] * 3,
+        out_specs=[whole_block(VMEM)] * n_mp,
+        scratch_shapes=[
+            pltpu.VMEM((n_grp * block, LANES), jnp.float32),
+            pltpu.VMEM((n_grp * block, LANES), jnp.float32),
+            pltpu.VMEM((rows_here * heads_here * n_mp, LANES), jnp.float32),
+            pltpu.VMEM((rows_here * 2 * kv_heads, LANES), jnp.float32),
+            pltpu.VMEM((n_mp, packed_rows, LANES), jnp.float32),
+        ],
+        compiler_params=pltpu.CompilerParams(vmem_limit_bytes=16 << 20),
+        name="attend",
+    )(
+        row_order,
+        stale_rows,
+        lengths,
+        held,
+        key_cache.reshape(rows_here, places, head_size),
+        value_cache.reshape(rows_here, places, head_size),
+    )
+    pieces = [partial_out[0]] + [
+        lax.ppermute(partial_out[k], "mp", [(i, i ^ k) for i in range(n_mp)]) for k in range(1, n_mp)
+    ]
+    return pl.pallas_call(
+        join_kernel,
+        out_shape=bf16((rows_here, heads_here, head_size)),
+        in_specs=[whole_block(VMEM)] * n_mp,
+        out_specs=whole_block(VMEM),
+        compiler_params=pltpu.CompilerParams(vmem_limit_bytes=4 << 20),
+        name="join",
+    )(*pieces)
+
+
+def fits(sizes, old_q, old_kv, fresh_q, key_cache):
+    n_grp, n_rep, n_mp = sizes
+    heads_here, head_size = old_q.shape[1:]
+    slots_here = old_kv.shape[1]
+    rows_here, _, kv_heads, _ = key_cache.shape
+    return (
+        head_size == LANES
+        and slots_here == n_grp
+        and heads_here == n_grp * n_grp
+        and fresh_q.shape[2] * n_grp == head_size
+        and n_grp & (n_grp - 1) == 0
+        and n_mp & (n_mp - 1) == 0
+        and heads_here * n_mp == SUBLANES * kv_heads
+        and heads_here % SUBLANES == 0
+        and slots_here * n_mp == 2 * kv_heads
+        and n_mp * rows_here * (n_grp + 1) % SUBLANES == 0
+        and LANES % (2 * rows_here) == 0
+        and n_grp * n_rep * rows_here % (2 * SUBLANES) == 0
+    )
+
+
+def local(sizes, *args):
+    old_q, old_kv, fresh_q, key_cache = args[4], args[5], args[6], args[8]
+    return (close if fits(sizes, old_q, old_kv, fresh_q, key_cache) else plain)(sizes, *args)
+
+
 def solution(mesh):
     sizes = tuple(mesh.shape[a] for a in AXES)
     return jax.shard_map(
-        functools.partial(plain, sizes),
+        functools.partial(local, sizes),
         mesh=mesh,
         in_specs=(
             P("grp", "rep"),

time: 63 us -> 37.2 us (0.59)
  local copies, waits for them, and re-layouts: 19.1 us -> 1.44 us
  Pallas kernels: 0 us -> 9.6 us
  matrix products: 7.41 us -> 0 us
  other arithmetic: 6.09 us -> 0 us
  waiting for transfers between devices: 8 us -> 4.29 us
  starting transfers between devices: 6.19 us -> 7.63 us
  blocking collectives: 15.4 us -> 14 us
    dynamic_slice x2 -> x0, local copies, waits for them, and re-layouts: 12.6 us -> none  [the longest x1 10 us: plain(): cut(old_q)]
    pallas_call x0 -> x5, Pallas kernels: none -> 9.6 us  [the longest x1 2.94 us: close(): pl.pallas_call(functools.partial(project_kernel, n_rep, n_mp), out_shape=...]
    all_to_all x1 -> x0, waiting for transfers between devices: 8 us -> none  [plain(): held = lax.all_to_all(terms, AXES, 0, 0, tiled=True)]
    ppermute x0 -> x6, starting transfers between devices: none -> 7.63 us  [the longest x3 4.45 us: close(): lax.ppermute(partial_out[k], 'mp', [(i, i ^ k) for i in range(n_mp)])]
    dot_general x6 -> x0, matrix products: 7.41 us -> none  [the longest x4 6.65 us: project(): jnp.einsum('bf,fhd->bhd', features, w, preferred_element_type=jnp.float32)]
    all_gather x1 -> x0, blocking collectives: 6.56 us -> none  [plain(): lax.all_gather(slot_order(inputs, stale_rows, row_order), 'grp', axis=0,...]
    all_to_all x1 -> x0, starting transfers between devices: 6.19 us -> none  [plain(): held = lax.all_to_all(terms, AXES, 0, 0, tiled=True)]
    all_to_all x1, blocking collectives: 8.89 us -> 14 us  [close(): lax.all_to_all(terms.reshape(devices, 1, rows_here * parts * head_size),...]
  transfers between devices with their start and end apart: 1 -> 6, of which waited for: 1 -> 3; matrix products, arithmetic and copies ran while one was open for 0% -> 0% of each run, Pallas kernels for 0% -> 6%
where the time goes in v2:
time: 37.2 us; the launch traced here: 37 us
  blocking collectives  14 us (38%)
  Pallas kernels  9.6 us (26%)
  starting transfers between devices  7.63 us (21%)
  waiting for transfers between devices  4.29 us (12%)
  local copies, waits for them, and re-layouts  1.44 us (4%)
    all_to_all x1, blocking collectives, close(): lax.all_to_all(terms.reshape(devices, 1, rows_here * parts * head_size),...  14 us
    ppermute x3, starting transfers between devices, close(): lax.ppermute(partial_out[k], 'mp', [(i, i ^ k) for i in range(n_mp)])  4.45 us
    ppermute x3, starting transfers between devices, exchanged(): lax.ppermute(value, axis, [(i, i ^ k) for i in range(count)])  3.18 us
    ppermute x3, waiting for transfers between devices, close(): lax.ppermute(partial_out[k], 'mp', [(i, i ^ k) for i in range(n_mp)])  3.15 us
    pallas_call x1, Pallas kernels, close(): pl.pallas_call(functools.partial(project_kernel, n_rep, n_mp), out_shape=...  2.94 us
    pallas_call x1, Pallas kernels, close(): pl.pallas_call(load_kernel, out_shape=share, in_specs=[whole_block(HBM)],...  2.36 us
    pallas_call x1, Pallas kernels, close(): pl.pallas_call(functools.partial(attend_kernel, sizes, 1.0 / math.sqrt(he...  2.09 us
    pallas_call x1, Pallas kernels, close(): pl.pallas_call(order_kernel, out_shape=bf16((group_rows, part_width + LAN...  1.45 us
  transfers between devices with their start and end apart: 6, of which 3 were waited for; matrix products, arithmetic and copies ran while one was open for 0% of the time, Pallas kernels for 6%

profile of v2, /device:TPU:0, one launch (start us, length us, event | category | flops | bytes accessed | tf_op | source)
XLA Modules:
  0.0 37.0 jit_solution(17837984814618024465)
XLA Ops:
  0.0 1.4 %order.2.refs_0_ = bf16[4,4224]{1,0:T(4,128)(2,1)} custom-call(s32[4]{0:T(128)} %order.3, s32[4]{0:T(128)} %stale.1, bf16[4,4096]{1,0:T(4,128)(2,1)} %rows_in.1), custom_call_target="tpu_custom_call" | custom-call | bytes 33554432 | tf_op jit(solution)/shard_map/order/pallas_call | solution.py:298
  1.5 2.5 %collective-permute-start.2 = (bf16[4,4224]{1,0:T(4,128)(2,1)}, bf16[4,4224]{1,0:T(4,128)(2,1)S(1)}, u32[]{:S(2)}, u32[]{:S(2)}) collective-permute-start(bf16[4,4224]{1,0:T(4,128)(2,1)} %order.2.refs_0_), channel_id=1, source_target_pairs={{0,24},{8,16},{16,8},{24,0},{1,25},{9,17},{17,9},{25,1},{2,26},{10... | collective-permute-start | bytes 101384 | tf_op jit(solution)/shard_map/ppermute | solution.py:281
  4.0 0.6 %collective-permute-start.1 = (bf16[4,4224]{1,0:T(4,128)(2,1)}, bf16[4,4224]{1,0:T(4,128)(2,1)S(1)}, u32[]{:S(2)}, u32[]{:S(2)}) collective-permute-start(bf16[4,4224]{1,0:T(4,128)(2,1)} %order.2.refs_0_), channel_id=1, source_target_pairs={{0,16},{8,24},{16,0},{24,8},{1,17},{9,25},{17,1},{25,9},{2,18},{10... | collective-permute-start | bytes 101384 | tf_op jit(solution)/shard_map/ppermute | solution.py:281
  4.6 0.0 collective-permute-start
  4.6 0.0 copy-start
  4.6 0.0 copy-start.1
  4.6 0.0 copy-start.2
  4.6 2.4 %load.1 = bf16[4096,4,128]{2,1,0:T(4,128)(2,1)S(1)} custom-call(bf16[4096,4,4,128]{3,2,1,0:T(4,128)(2,1)} %bitcast.21), custom_call_target="tpu_custom_call" | custom-call | bytes 8388608 | tf_op jit(solution)/shard_map/load/pallas_call | solution.py:315
  7.0 0.0 collective-permute-done.2.refs_3_
  7.0 1.1 %collective-permute-done.1.refs_2_ = bf16[4,4224]{1,0:T(4,128)(2,1)S(1)} collective-permute-done((bf16[4,4224]{1,0:T(4,128)(2,1)}, bf16[4,4224]{1,0:T(4,128)(2,1)S(1)}, u32[]{:S(2)}, u32[]{:S(2)}) %collective-permute-start.1) | collective-permute-done | bytes 33824 | tf_op jit(solution)/shard_map/ppermute | solution.py:281
  8.2 0.0 collective-permute-done.refs_1_
  8.2 0.0 copy-done
  8.2 1.2 %copy-done.1 = bf16[4096,16,32]{0,2,1:T(8,128)(2,1)S(1)} copy-done((bf16[4096,16,32]{0,2,1:T(8,128)(2,1)S(1)}, bf16[4096,16,32]{0,2,1:T(8,128)(2,1)}, u32[]{:S(2)}) %copy-start.1) | copy-done | bytes 4194328
  9.4 0.2 copy-done.2
  9.6 0.0 copy-done.5
  9.6 0.0 copy-start.7
  9.6 0.0 copy-start.8
  9.6 2.9 %project.1 = f32[8,40,128]{2,1,0:T(8,128)S(1)} custom-call(bf16[4,4224]{1,0:T(4,128)(2,1)S(1)} %copy-done.5, bf16[4,4224]{1,0:T(4,128)(2,1)S(1)} %collective-permute-done.refs_1_, bf16[4,4224]{1,0:T(4,128)(2,1)S(1)} %collective-permute-done.1.refs_2_, bf16[4,4224]{1,0:T(4,128)(2,1)S(1)} %collective-permute-done.2.refs_3_, bf16[16384,128]{1,0:T(8,128)(2,1)S(1)} %bitcast.13, ...), custom_call_target="tpu_custom_call" | custom-call | tf_op jit(solution)/shard_map/project/pallas_call | solution.py:331
  12.6 14.0 %all_to_all.5 = f32[32,1,1280]{2,1,0:T(1,128)S(1)} all-to-all(f32[32,1,1280]{2,1,0:T(1,128)S(1)} %bitcast.20), channel_id=1, replica_groups=mesh['grp'=4,'rep'=2,'mp'=4] {'grp','rep','mp'}, dimensions={0} | all-to-all | bytes 327680 | tf_op jit(solution)/shard_map/all_to_all | solution.py:344
  26.5 0.0 copy-done.3
  26.5 0.0 copy-done.4
  26.6 0.0 copy-done.6
  26.6 0.0 copy-done.7
  26.6 0.0 copy-done.8
  26.6 2.1 %attend.1 = (f32[48,128]{1,0:T(8,128)S(1)}, f32[48,128]{1,0:T(8,128)S(1)}, f32[48,128]{1,0:T(8,128)S(1)}, f32[48,128]{1,0:T(8,128)S(1)}) custom-call(s32[4]{0:T(128)S(1)} %copy-done.6, s32[4]{0:T(128)S(1)} %copy-done.7, s32[2]{0:T(128)S(1)} %copy-done.8, f32[8,40,128]{2,1,0:T(8,128)S(1)} %bitcast.19, bf16[2,2048,128]{2,1,0:T(8,128)(2,1)S(1)} %bitcast.17, ...), custom_call_target="tpu_custom_call" | custom-call | tf_op jit(solution)/shard_map/attend/pallas_call | solution.py:348
  28.7 1.3 %collective-permute-start.3 = (f32[48,128]{1,0:T(8,128)S(1)}, f32[48,128]{1,0:T(8,128)S(1)}, u32[]{:S(2)}, u32[]{:S(2)}) collective-permute-start(f32[48,128]{1,0:T(8,128)S(1)} %get-tuple-element.10), channel_id=1, source_target_pairs={{0,1},{1,0},{2,3},{3,2},{4,5},{5,4},{6,7},{7,6},{8,9},{9,8},{10,11... | collective-permute-start | bytes 73736 | tf_op jit(solution)/shard_map/ppermute | solution.py:371
  29.9 0.7 %collective-permute-start.4 = (f32[48,128]{1,0:T(8,128)S(1)}, f32[48,128]{1,0:T(8,128)S(1)}, u32[]{:S(2)}, u32[]{:S(2)}) collective-permute-start(f32[48,128]{1,0:T(8,128)S(1)} %get-tuple-element.11), channel_id=1, source_target_pairs={{0,2},{1,3},{2,0},{3,1},{4,6},{5,7},{6,4},{7,5},{8,10},{9,11},{10,... | collective-permute-start | bytes 73736 | tf_op jit(solution)/shard_map/ppermute | solution.py:371
  30.6 2.5 %collective-permute-start.5 = (f32[48,128]{1,0:T(8,128)S(1)}, f32[48,128]{1,0:T(8,128)S(1)}, u32[]{:S(2)}, u32[]{:S(2)}) collective-permute-start(f32[48,128]{1,0:T(8,128)S(1)} %get-tuple-element.12), channel_id=1, source_target_pairs={{0,3},{1,2},{2,1},{3,0},{4,7},{5,6},{6,5},{7,4},{8,11},{9,10},{10,... | collective-permute-start | bytes 73736 | tf_op jit(solution)/shard_map/ppermute | solution.py:371
  33.1 0.0 collective-permute-done.3.refs_1_
  33.1 1.5 %collective-permute-done.4.refs_2_ = f32[48,128]{1,0:T(8,128)S(1)} collective-permute-done((f32[48,128]{1,0:T(8,128)S(1)}, f32[48,128]{1,0:T(8,128)S(1)}, u32[]{:S(2)}, u32[]{:S(2)}) %collective-permute-start.4) | collective-permute-done | bytes 24608 | tf_op jit(solution)/shard_map/ppermute | solution.py:371
  34.7 1.6 %collective-permute-done.5.refs_3_ = f32[48,128]{1,0:T(8,128)S(1)} collective-permute-done((f32[48,128]{1,0:T(8,128)S(1)}, f32[48,128]{1,0:T(8,128)S(1)}, u32[]{:S(2)}, u32[]{:S(2)}) %collective-permute-start.5) | collective-permute-done | bytes 24608 | tf_op jit(solution)/shard_map/ppermute | solution.py:371
  36.3 0.8 %join.1 = bf16[2,16,128]{2,1,0:T(8,128)(2,1)} custom-call(f32[48,128]{1,0:T(8,128)S(1)} %get-tuple-element.9.refs_0_, f32[48,128]{1,0:T(8,128)S(1)} %collective-permute-done.3.refs_1_, f32[48,128]{1,0:T(8,128)S(1)} %collective-permute-done.4.refs_2_, f32[48,128]{1,0:T(8,128)S(1)} %collective-permute-done.5.refs_3_), custom_call_target="tpu_custom_call" | custom-call | tf_op jit(solution)/shard_map/join/pallas_call | solution.py:373
  (4 shorter events, 0.0 us)
Async XLA Ops:
  1.5 5.6 %collective-permute-start.2 = (bf16[4,4224]{1,0:T(4,128)(2,1)}, bf16[4,4224]{1,0:T(4,128)(2,1)S(1)}, u32[]{:S(2)}, u32[]{:S(2)}) collective-permute-start(bf16[4,4224]{1,0:T(4,128)(2,1)} %order.2.refs_0_), channel_id=1, source_target_pairs={{0,24},{8,16},{16,8},{24,0},{1,25},{9,17},{17,9},{25,1},{2,26},{10... | collective-permute-start | bytes 101384 | tf_op jit(solution)/shard_map/ppermute | solution.py:281
  4.0 4.2 %collective-permute-start.1 = (bf16[4,4224]{1,0:T(4,128)(2,1)}, bf16[4,4224]{1,0:T(4,128)(2,1)S(1)}, u32[]{:S(2)}, u32[]{:S(2)}) collective-permute-start(bf16[4,4224]{1,0:T(4,128)(2,1)} %order.2.refs_0_), channel_id=1, source_target_pairs={{0,16},{8,24},{16,0},{24,8},{1,17},{9,25},{17,1},{25,9},{2,18},{10... | collective-permute-start | bytes 101384 | tf_op jit(solution)/shard_map/ppermute | solution.py:281
  4.6 3.6 %collective-permute-start = (bf16[4,4224]{1,0:T(4,128)(2,1)}, bf16[4,4224]{1,0:T(4,128)(2,1)S(1)}, u32[]{:S(2)}, u32[]{:S(2)}) collective-permute-start(bf16[4,4224]{1,0:T(4,128)(2,1)} %order.2.refs_0_), channel_id=1, source_target_pairs={{0,8},{8,0},{16,24},{24,16},{1,9},{9,1},{17,25},{25,17},{2,10},{10... | collective-permute-start | bytes 101384 | tf_op jit(solution)/shard_map/ppermute | solution.py:281
  4.6 3.5 %copy-start = (bf16[4096,4,128]{2,1,0:T(4,128)(2,1)S(1)}, bf16[4096,4,128]{2,1,0:T(4,128)(2,1)}, u32[]{:S(2)}) copy-start(bf16[4096,4,128]{2,1,0:T(4,128)(2,1)} %param.15) | copy-start | bytes 12582916
  4.6 4.7 %copy-start.1 = (bf16[4096,16,32]{0,2,1:T(8,128)(2,1)S(1)}, bf16[4096,16,32]{0,2,1:T(8,128)(2,1)}, u32[]{:S(2)}) copy-start(bf16[4096,16,32]{0,2,1:T(8,128)(2,1)} %param.16) | copy-start | bytes 12582916
  4.6 4.9 %copy-start.2 = (bf16[4096,4,32]{0,2,1:T(8,128)(2,1)S(1)}, bf16[4096,4,32]{0,2,1:T(8,128)(2,1)}, u32[]{:S(2)}) copy-start(bf16[4096,4,32]{0,2,1:T(8,128)(2,1)} %param.17) | copy-start | bytes 3145732
  4.6 4.9 %copy-start.5 = (bf16[4,4224]{1,0:T(4,128)(2,1)S(1)}, bf16[4,4224]{1,0:T(4,128)(2,1)}, u32[]{:S(2)}) copy-start(bf16[4,4224]{1,0:T(4,128)(2,1)} %order.2.refs_0_) | copy-start | bytes 101380
  9.6 17.0 %copy-start.3 = (bf16[2,256,8,128]{3,2,1,0:T(8,128)(2,1)S(1)}, bf16[2,256,8,128]{3,2,1,0:T(8,128)(2,1)}, u32[]{:S(2)}) copy-start(bf16[2,256,8,128]{3,2,1,0:T(8,128)(2,1)} %param.18) | copy-start | bytes 3145732
  9.6 17.0 %copy-start.4 = (bf16[2,256,8,128]{3,2,1,0:T(8,128)(2,1)S(1)}, bf16[2,256,8,128]{3,2,1,0:T(8,128)(2,1)}, u32[]{:S(2)}) copy-start(bf16[2,256,8,128]{3,2,1,0:T(8,128)(2,1)} %param.19) | copy-start | bytes 3145732
  9.6 17.0 %copy-start.6 = (s32[4]{0:T(128)S(1)}, s32[4]{0:T(128)}, u32[]{:S(2)}) copy-start(s32[4]{0:T(128)} %order.3) | copy-start | bytes 52
  9.6 17.0 %copy-start.7 = (s32[4]{0:T(128)S(1)}, s32[4]{0:T(128)}, u32[]{:S(2)}) copy-start(s32[4]{0:T(128)} %stale.1) | copy-start | bytes 52
  9.6 17.0 %copy-start.8 = (s32[2]{0:T(128)S(1)}, s32[2]{0:T(128)}, u32[]{:S(2)}) copy-start(s32[2]{0:T(128)} %lengths.1) | copy-start | bytes 28
  28.7 4.5 %collective-permute-start.3 = (f32[48,128]{1,0:T(8,128)S(1)}, f32[48,128]{1,0:T(8,128)S(1)}, u32[]{:S(2)}, u32[]{:S(2)}) collective-permute-start(f32[48,128]{1,0:T(8,128)S(1)} %get-tuple-element.10), channel_id=1, source_target_pairs={{0,1},{1,0},{2,3},{3,2},{4,5},{5,4},{6,7},{7,6},{8,9},{9,8},{10,11... | collective-permute-start | bytes 73736 | tf_op jit(solution)/shard_map/ppermute | solution.py:371
  29.9 4.7 %collective-permute-start.4 = (f32[48,128]{1,0:T(8,128)S(1)}, f32[48,128]{1,0:T(8,128)S(1)}, u32[]{:S(2)}, u32[]{:S(2)}) collective-permute-start(f32[48,128]{1,0:T(8,128)S(1)} %get-tuple-element.11), channel_id=1, source_target_pairs={{0,2},{1,3},{2,0},{3,1},{4,6},{5,7},{6,4},{7,5},{8,10},{9,11},{10,... | collective-permute-start | bytes 73736 | tf_op jit(solution)/shard_map/ppermute | solution.py:371
  30.6 5.6 %collective-permute-start.5 = (f32[48,128]{1,0:T(8,128)S(1)}, f32[48,128]{1,0:T(8,128)S(1)}, u32[]{:S(2)}, u32[]{:S(2)}) collective-permute-start(f32[48,128]{1,0:T(8,128)S(1)} %get-tuple-element.12), channel_id=1, source_target_pairs={{0,3},{1,2},{2,1},{3,0},{4,7},{5,6},{6,5},{7,4},{8,11},{9,10},{10,... | collective-permute-start | bytes 73736 | tf_op jit(solution)/shard_map/ppermute | solution.py:371

commit v3 on v2

--- a/solution.py
+++ b/solution.py
@@ -88,15 +88,18 @@
 HBM = pltpu.MemorySpace.HBM
 VMEM = pltpu.MemorySpace.VMEM
 SMEM = pltpu.MemorySpace.SMEM
-ROOMY = 67_043_328
+ROOMY = 57000000
+LOAD_LIMIT = 40_000_000
+PROJECT_LIMIT = 24_000_000
 START_BYTES = 32 << 20
+SPANS = 4
 
 
 def whole_block(space):
     return pl.BlockSpec(memory_space=space)
 
 
-def order_kernel(order_in, stale_in, rows_in, moved, order, stale, rows, sems):
+def order_kernel(order_in, stale_in, rows_in, _, moved, order, stale, rows, sems):
     pairs = ((order_in, order), (stale_in, stale), (rows_in, rows))
     copies = [pltpu.make_async_copy(a, b, sems.at[n]) for n, (a, b) in enumerate(pairs)]
     for copy in copies:
@@ -115,7 +118,8 @@
     moved[:, width:] = flags.astype(moved.dtype)
 
 
-def load_kernel(old_q, near, sem):
+def load_kernel(old_q, *refs):
+    near, sem = refs[-2:]
     copy = pltpu.make_async_copy(old_q.at[:, lax.axis_index("grp")], near, sem)
     copy.start()
     copy.wait()
@@ -141,24 +145,36 @@
     wide = jnp.dot(stacked, spread, preferred_element_type=jnp.float32).astype(jnp.bfloat16)
     lane = lax.broadcasted_iota(jnp.int32, (1, spread_width), 1) % per_row
     picks = [jnp.where(lane == h, 1.0, 0.0).astype(jnp.bfloat16) for h in range(per_row)]
-    old = jnp.zeros((per_row * rows, 2 * LANES), jnp.float32)
-    for c in range(chunks):
-        piece = wide[c * rows : (c + 1) * rows]
-        left = jnp.concatenate([piece * pick for pick in picks], axis=0)
-        span = slice(c * spread_width, (c + 1) * spread_width)
-        right = jnp.concatenate([old_q[span, :], old_kv[span, :]], axis=1)
-        old = old + jnp.dot(left, right, preferred_element_type=jnp.float32)
+
+    def add(weights):
+        half = chunks // 2
+        sums = []
+        for side in range(2):
+            total = 0
+            for c in range(side * half, (side + 1) * half, SPANS):
+                left = []
+                for u in range(c, c + SPANS):
+                    piece = wide[u * rows : (u + 1) * rows]
+                    left.append(jnp.concatenate([piece * pick for pick in picks], axis=0))
+                left = jnp.concatenate(left, axis=1)
+                right = weights[c * spread_width : (c + SPANS) * spread_width, :]
+                total = total + jnp.dot(left, right, preferred_element_type=jnp.float32)
+            sums.append(total)
+        return sums[0] + sums[1]
+
+    across = (((1,), (1,)), ((), ()))
+    kept_kv = add(old_kv)
     values = features[:, :part_width]
-    across = (((1,), (1,)), ((), ()))
-    new_q = lax.dot_general(values, fresh_q[...], across, preferred_element_type=jnp.float32)
-    new_kv = lax.dot_general(values, fresh_kv[...], across, preferred_element_type=jnp.float32)
+    new_q = lax.dot_general(fresh_q[...], values, across, preferred_element_type=jnp.float32).T
+    new_kv = lax.dot_general(fresh_kv[...], values, across, preferred_element_type=jnp.float32).T
+    kept_q = add(old_q)
     stale = features[:, part_width : part_width + 1].astype(jnp.float32) == 1.0
     for j in range(per_row):
         span = slice(j * LANES, (j + 1) * LANES)
-        staged[j * rows : (j + 1) * rows, :] = jnp.where(stale, old[j * rows : (j + 1) * rows, :LANES], new_q[:, span])
-    kept = old[:rows, LANES:]
+        staged[j * rows : (j + 1) * rows, :] = jnp.where(stale, kept_q[j * rows : (j + 1) * rows], new_q[:, span])
+    kept = kept_kv[:rows]
     for h in range(1, per_row):
-        kept = jnp.where(mine == h, old[h * rows : (h + 1) * rows, LANES:], kept)
+        kept = jnp.where(mine == h, kept_kv[h * rows : (h + 1) * rows], kept)
     staged[per_row * rows :, :] = jnp.where(stale, kept, new_kv)
     parts = per_row + 1
     rows_here = group_rows // n_rep
@@ -298,7 +314,7 @@
     moved = pl.pallas_call(
         order_kernel,
         out_shape=bf16((group_rows, part_width + LANES)),
-        in_specs=[whole_block(HBM)] * 3,
+        in_specs=[whole_block(HBM)] * 4,
         out_specs=whole_block(VMEM),
         scratch_shapes=[
             pltpu.SMEM((group_rows,), jnp.int32),
@@ -309,24 +325,22 @@
         compiler_params=pltpu.CompilerParams(vmem_limit_bytes=ROOMY),
         cost_estimate=pl.CostEstimate(flops=0, bytes_accessed=START_BYTES, transcendentals=0),
         name="order",
-    )(row_order, stale_rows, inputs)
+    )(row_order, stale_rows, inputs, old_q)
     gathered = exchanged(moved, "grp", n_grp)
-    share = bf16((part_width, shares, head_size))
-    near_q = pl.pallas_call(
-        load_kernel,
-        out_shape=share,
-        in_specs=[whole_block(HBM)],
-        out_specs=whole_block(pl.ANY),
-        scratch_shapes=[pltpu.SemaphoreType.DMA],
-        compiler_params=pltpu.CompilerParams(vmem_limit_bytes=40 << 20),
-        cost_estimate=pl.CostEstimate(flops=0, bytes_accessed=4 * math.prod(share.shape), transcendentals=0),
-        name="load",
-    )(old_q.reshape(part_width, n_grp, shares, head_size))
     near = (
         old_kv.reshape(part_width * n_grp, head_size),
         jnp.transpose(fresh_q, (1, 2, 0)).reshape(heads_here * slice_here, part_width),
         jnp.transpose(fresh_kv, (1, 2, 0)).reshape(n_grp * slice_here, part_width),
     )
+    near_q = pl.pallas_call(
+        load_kernel,
+        out_shape=bf16((part_width, shares, head_size)),
+        in_specs=[whole_block(HBM)] + [whole_block(VMEM)] * 3,
+        out_specs=whole_block(pl.ANY),
+        scratch_shapes=[pltpu.SemaphoreType.DMA],
+        compiler_params=pltpu.CompilerParams(vmem_limit_bytes=LOAD_LIMIT),
+        name="load",
+    )(old_q.reshape(part_width, n_grp, shares, head_size), *near)
     block = n_mp * rows_here * parts
     terms = pl.pallas_call(
         functools.partial(project_kernel, n_rep, n_mp),
@@ -337,7 +351,7 @@
             pltpu.VMEM((rows, part_width + LANES), jnp.bfloat16),
             pltpu.VMEM((rows * parts, LANES), jnp.float32),
         ],
-        compiler_params=pltpu.CompilerParams(vmem_limit_bytes=24 << 20),
+        compiler_params=pltpu.CompilerParams(vmem_limit_bytes=PROJECT_LIMIT),
         name="project",
     )(*gathered, near_q.reshape(part_width * shares, head_size), *near)
     devices = n_grp * n_rep * n_mp
@@ -368,7 +382,7 @@
         value_cache.reshape(rows_here, places, head_size),
     )
     pieces = [partial_out[0]] + [
-        lax.ppermute(partial_out[k], "mp", [(i, i ^ k) for i in range(n_mp)]) for k in range(1, n_mp)
+        lax.ppermute(partial_out[k], "mp", [(i, i ^ k) for i in range(n_mp)]) for k in range(n_mp - 1, 0, -1)
     ]
     return pl.pallas_call(
         join_kernel,
@@ -398,6 +412,7 @@
         and n_mp * rows_here * (n_grp + 1) % SUBLANES == 0
         and LANES % (2 * rows_here) == 0
         and n_grp * n_rep * rows_here % (2 * SUBLANES) == 0
+        and old_q.shape[0] % (2 * SPANS * LANES) == 0
     )
 
 

time: 37.2 us -> 34.3 us (0.922)
  local copies, waits for them, and re-layouts: 1.44 us -> 0.04 us
  waiting for transfers between devices: 4.29 us -> 3.42 us
  blocking collectives: 14 us -> 13.2 us
    unnamed x18, local copies, waits for them, and re-layouts: 1.44 us -> 0.04 us
    ppermute x3, waiting for transfers between devices: 3.15 us -> 2.13 us  [close(): lax.ppermute(partial_out[k], 'mp', [(i, i ^ k) for i in range(n_mp)])]
    all_to_all x1, blocking collectives: 14 us -> 13.2 us  [close(): lax.all_to_all(terms.reshape(devices, 1, rows_here * parts * head_size),...]
  transfers between devices with their start and end apart: 6 -> 6, of which waited for: 3 -> 4; matrix products, arithmetic and copies ran while one was open for 0% -> 0% of each run, Pallas kernels for 6% -> 6%
where the time goes in v3:
time: 34.3 us; the launch traced here: 34.2 us
  blocking collectives  13.2 us (38%)
  Pallas kernels  9.72 us (28%)
  starting transfers between devices  7.64 us (22%)
  waiting for transfers between devices  3.42 us (10%)
    all_to_all x1, blocking collectives, close(): lax.all_to_all(terms.reshape(devices, 1, rows_here * parts * head_size),...  13.2 us
    ppermute x3, starting transfers between devices, close(): lax.ppermute(partial_out[k], 'mp', [(i, i ^ k) for i in range(n_mp)])  4.45 us
    ppermute x3, starting transfers between devices, exchanged(): lax.ppermute(value, axis, [(i, i ^ k) for i in range(count)])  3.19 us
    pallas_call x1, Pallas kernels, close(): pl.pallas_call(functools.partial(project_kernel, n_rep, n_mp), out_shape=...  3.07 us
    pallas_call x1, Pallas kernels, close(): pl.pallas_call(load_kernel, out_shape=bf16((part_width, shares, head_size...  2.21 us
    ppermute x3, waiting for transfers between devices, close(): lax.ppermute(partial_out[k], 'mp', [(i, i ^ k) for i in range(n_mp)])  2.13 us
    pallas_call x1, Pallas kernels, close(): pl.pallas_call(functools.partial(attend_kernel, sizes, 1.0 / math.sqrt(he...  2.07 us
    pallas_call x1, Pallas kernels, close(): pl.pallas_call(order_kernel, out_shape=bf16((group_rows, part_width + LAN...  1.6 us
  transfers between devices with their start and end apart: 6, of which 4 were waited for; matrix products, arithmetic and copies ran while one was open for 0% of the time, Pallas kernels for 6%

profile of v3, /device:TPU:0, one launch (start us, length us, event | category | flops | bytes accessed | tf_op | source)
XLA Modules:
  0.0 34.2 jit_solution(8122585019239611399)
XLA Ops:
  0.0 0.0 copy-start.2
  0.0 1.6 %order.2.refs_0_ = bf16[4,4224]{1,0:T(4,128)(2,1)} custom-call(s32[4]{0:T(128)} %order.3, s32[4]{0:T(128)} %stale.1, bf16[4,4096]{1,0:T(4,128)(2,1)} %rows_in.1, bf16[4096,16,128]{2,1,0:T(8,128)(2,1)} %_.1), custom_call_target="tpu_custom_call" | custom-call | bytes 33554432 | tf_op jit(solution)/shard_map/order/pallas_call | solution.py:314
  1.6 2.5 %collective-permute-start.2 = (bf16[4,4224]{1,0:T(4,128)(2,1)}, bf16[4,4224]{1,0:T(4,128)(2,1)S(1)}, u32[]{:S(2)}, u32[]{:S(2)}) collective-permute-start(bf16[4,4224]{1,0:T(4,128)(2,1)} %order.2.refs_0_), channel_id=1, source_target_pairs={{0,24},{8,16},{16,8},{24,0},{1,25},{9,17},{17,9},{25,1},{2,26},{10... | collective-permute-start | bytes 101384 | tf_op jit(solution)/shard_map/ppermute | solution.py:297
  4.1 0.6 %collective-permute-start.1 = (bf16[4,4224]{1,0:T(4,128)(2,1)}, bf16[4,4224]{1,0:T(4,128)(2,1)S(1)}, u32[]{:S(2)}, u32[]{:S(2)}) collective-permute-start(bf16[4,4224]{1,0:T(4,128)(2,1)} %order.2.refs_0_), channel_id=1, source_target_pairs={{0,16},{8,24},{16,0},{24,8},{1,17},{9,25},{17,1},{25,9},{2,18},{10... | collective-permute-start | bytes 101384 | tf_op jit(solution)/shard_map/ppermute | solution.py:297
  4.8 0.0 collective-permute-start
  4.8 0.0 copy-done.2
  4.8 0.0 copy-done.1
  4.8 0.0 copy-done
  4.8 2.2 %load.1 = bf16[4096,4,128]{2,1,0:T(4,128)(2,1)S(1)} custom-call(bf16[4096,4,4,128]{3,2,1,0:T(4,128)(2,1)} %bitcast.24, bf16[16384,128]{1,0:T(8,128)(2,1)S(1)} %bitcast.13, bf16[512,4096]{1,0:T(8,128)(2,1)S(1)} %bitcast.15, bf16[128,4096]{1,0:T(8,128)(2,1)S(1)} %bitcast.18), custom_call_target="tpu_custom_call" | custom-call | tf_op jit(solution)/shard_map/load/pallas_call | solution.py:335
  7.0 0.0 collective-permute-done.2.refs_3_
  7.0 1.3 %collective-permute-done.1.refs_2_ = bf16[4,4224]{1,0:T(4,128)(2,1)S(1)} collective-permute-done((bf16[4,4224]{1,0:T(4,128)(2,1)}, bf16[4,4224]{1,0:T(4,128)(2,1)S(1)}, u32[]{:S(2)}, u32[]{:S(2)}) %collective-permute-start.1) | collective-permute-done | bytes 33824 | tf_op jit(solution)/shard_map/ppermute | solution.py:297
  8.3 0.0 collective-permute-done.refs_1_
  8.3 0.0 copy-done.5
  8.3 0.0 copy-start.4
  8.3 0.0 copy-start.6
  8.4 0.0 copy-start.7
  8.4 0.0 copy-start.8
  8.4 3.1 %project.1 = f32[8,40,128]{2,1,0:T(8,128)S(1)} custom-call(bf16[4,4224]{1,0:T(4,128)(2,1)S(1)} %copy-done.5, bf16[4,4224]{1,0:T(4,128)(2,1)S(1)} %collective-permute-done.refs_1_, bf16[4,4224]{1,0:T(4,128)(2,1)S(1)} %collective-permute-done.1.refs_2_, bf16[4,4224]{1,0:T(4,128)(2,1)S(1)} %collective-permute-done.2.refs_3_, bf16[16384,128]{1,0:T(8,128)(2,1)S(1)} %bitcast.17, ...), custom_call_target="tpu_custom_call" | custom-call | tf_op jit(solution)/shard_map/project/pallas_call | solution.py:345
  11.5 13.2 %all_to_all.5 = f32[32,1,1280]{2,1,0:T(1,128)S(1)} all-to-all(f32[32,1,1280]{2,1,0:T(1,128)S(1)} %bitcast.23), channel_id=1, replica_groups=mesh['grp'=4,'rep'=2,'mp'=4] {'grp','rep','mp'}, dimensions={0} | all-to-all | bytes 327680 | tf_op jit(solution)/shard_map/all_to_all | solution.py:358
  24.7 0.0 copy-done.3
  24.7 0.0 copy-done.4
  24.7 0.0 copy-done.6
  24.7 0.0 copy-done.7
  24.7 0.0 copy-done.8
  24.7 2.1 %attend.1 = (f32[48,128]{1,0:T(8,128)S(1)}, f32[48,128]{1,0:T(8,128)S(1)}, f32[48,128]{1,0:T(8,128)S(1)}, f32[48,128]{1,0:T(8,128)S(1)}) custom-call(s32[4]{0:T(128)S(1)} %copy-done.6, s32[4]{0:T(128)S(1)} %copy-done.7, s32[2]{0:T(128)S(1)} %copy-done.8, f32[8,40,128]{2,1,0:T(8,128)S(1)} %bitcast.22, bf16[2,2048,128]{2,1,0:T(8,128)(2,1)S(1)} %bitcast.20, ...), custom_call_target="tpu_custom_call" | custom-call | tf_op jit(solution)/shard_map/attend/pallas_call | solution.py:362
  26.8 1.4 %collective-permute-start.3 = (f32[48,128]{1,0:T(8,128)S(1)}, f32[48,128]{1,0:T(8,128)S(1)}, u32[]{:S(2)}, u32[]{:S(2)}) collective-permute-start(f32[48,128]{1,0:T(8,128)S(1)} %get-tuple-element.10), channel_id=1, source_target_pairs={{0,3},{1,2},{2,1},{3,0},{4,7},{5,6},{6,5},{7,4},{8,11},{9,10},{10,... | collective-permute-start | bytes 73736 | tf_op jit(solution)/shard_map/ppermute | solution.py:385
  28.2 1.3 %collective-permute-start.4 = (f32[48,128]{1,0:T(8,128)S(1)}, f32[48,128]{1,0:T(8,128)S(1)}, u32[]{:S(2)}, u32[]{:S(2)}) collective-permute-start(f32[48,128]{1,0:T(8,128)S(1)} %get-tuple-element.11), channel_id=1, source_target_pairs={{0,2},{1,3},{2,0},{3,1},{4,6},{5,7},{6,4},{7,5},{8,10},{9,11},{10,... | collective-permute-start | bytes 73736 | tf_op jit(solution)/shard_map/ppermute | solution.py:385
  29.5 1.7 %collective-permute-start.5 = (f32[48,128]{1,0:T(8,128)S(1)}, f32[48,128]{1,0:T(8,128)S(1)}, u32[]{:S(2)}, u32[]{:S(2)}) collective-permute-start(f32[48,128]{1,0:T(8,128)S(1)} %get-tuple-element.12), channel_id=1, source_target_pairs={{0,1},{1,0},{2,3},{3,2},{4,5},{5,4},{6,7},{7,6},{8,9},{9,8},{10,11... | collective-permute-start | bytes 73736 | tf_op jit(solution)/shard_map/ppermute | solution.py:385
  31.3 1.2 %collective-permute-done.3.refs_1_ = f32[48,128]{1,0:T(8,128)S(1)} collective-permute-done((f32[48,128]{1,0:T(8,128)S(1)}, f32[48,128]{1,0:T(8,128)S(1)}, u32[]{:S(2)}, u32[]{:S(2)}) %collective-permute-start.3) | collective-permute-done | bytes 24608 | tf_op jit(solution)/shard_map/ppermute | solution.py:385
  32.5 0.7 %collective-permute-done.4.refs_2_ = f32[48,128]{1,0:T(8,128)S(1)} collective-permute-done((f32[48,128]{1,0:T(8,128)S(1)}, f32[48,128]{1,0:T(8,128)S(1)}, u32[]{:S(2)}, u32[]{:S(2)}) %collective-permute-start.4) | collective-permute-done | bytes 24608 | tf_op jit(solution)/shard_map/ppermute | solution.py:385
  33.2 0.2 collective-permute-done.5.refs_3_
  33.4 0.8 %join.1 = bf16[2,16,128]{2,1,0:T(8,128)(2,1)} custom-call(f32[48,128]{1,0:T(8,128)S(1)} %get-tuple-element.9.refs_0_, f32[48,128]{1,0:T(8,128)S(1)} %collective-permute-done.3.refs_1_, f32[48,128]{1,0:T(8,128)S(1)} %collective-permute-done.4.refs_2_, f32[48,128]{1,0:T(8,128)S(1)} %collective-permute-done.5.refs_3_), custom_call_target="tpu_custom_call" | custom-call | tf_op jit(solution)/shard_map/join/pallas_call | solution.py:387
  (4 shorter events, 0.0 us)
Async XLA Ops:
  0.0 4.8 %copy-start.2 = (bf16[4096,4,32]{0,2,1:T(8,128)(2,1)S(1)}, bf16[4096,4,32]{0,2,1:T(8,128)(2,1)}, u32[]{:S(2)}) copy-start(bf16[4096,4,32]{0,2,1:T(8,128)(2,1)} %param.17) | copy-start | bytes 3145732
  0.0 4.8 %copy-start.1 = (bf16[4096,16,32]{0,2,1:T(8,128)(2,1)S(1)}, bf16[4096,16,32]{0,2,1:T(8,128)(2,1)}, u32[]{:S(2)}) copy-start(bf16[4096,16,32]{0,2,1:T(8,128)(2,1)} %param.16) | copy-start | bytes 12582916
  0.0 4.8 %copy-start = (bf16[4096,4,128]{2,1,0:T(4,128)(2,1)S(1)}, bf16[4096,4,128]{2,1,0:T(4,128)(2,1)}, u32[]{:S(2)}) copy-start(bf16[4096,4,128]{2,1,0:T(4,128)(2,1)} %param.15) | copy-start | bytes 12582916
  1.6 5.4 %collective-permute-start.2 = (bf16[4,4224]{1,0:T(4,128)(2,1)}, bf16[4,4224]{1,0:T(4,128)(2,1)S(1)}, u32[]{:S(2)}, u32[]{:S(2)}) collective-permute-start(bf16[4,4224]{1,0:T(4,128)(2,1)} %order.2.refs_0_), channel_id=1, source_target_pairs={{0,24},{8,16},{16,8},{24,0},{1,25},{9,17},{17,9},{25,1},{2,26},{10... | collective-permute-start | bytes 101384 | tf_op jit(solution)/shard_map/ppermute | solution.py:297
  4.1 4.2 %collective-permute-start.1 = (bf16[4,4224]{1,0:T(4,128)(2,1)}, bf16[4,4224]{1,0:T(4,128)(2,1)S(1)}, u32[]{:S(2)}, u32[]{:S(2)}) collective-permute-start(bf16[4,4224]{1,0:T(4,128)(2,1)} %order.2.refs_0_), channel_id=1, source_target_pairs={{0,16},{8,24},{16,0},{24,8},{1,17},{9,25},{17,1},{25,9},{2,18},{10... | collective-permute-start | bytes 101384 | tf_op jit(solution)/shard_map/ppermute | solution.py:297
  4.8 3.6 %collective-permute-start = (bf16[4,4224]{1,0:T(4,128)(2,1)}, bf16[4,4224]{1,0:T(4,128)(2,1)S(1)}, u32[]{:S(2)}, u32[]{:S(2)}) collective-permute-start(bf16[4,4224]{1,0:T(4,128)(2,1)} %order.2.refs_0_), channel_id=1, source_target_pairs={{0,8},{8,0},{16,24},{24,16},{1,9},{9,1},{17,25},{25,17},{2,10},{10... | collective-permute-start | bytes 101384 | tf_op jit(solution)/shard_map/ppermute | solution.py:297
  4.8 3.5 %copy-start.5 = (bf16[4,4224]{1,0:T(4,128)(2,1)S(1)}, bf16[4,4224]{1,0:T(4,128)(2,1)}, u32[]{:S(2)}) copy-start(bf16[4,4224]{1,0:T(4,128)(2,1)} %order.2.refs_0_) | copy-start | bytes 101380
  8.3 16.4 %copy-start.3 = (bf16[2,256,8,128]{3,2,1,0:T(8,128)(2,1)S(1)}, bf16[2,256,8,128]{3,2,1,0:T(8,128)(2,1)}, u32[]{:S(2)}) copy-start(bf16[2,256,8,128]{3,2,1,0:T(8,128)(2,1)} %param.18) | copy-start | bytes 3145732
  8.3 16.4 %copy-start.4 = (bf16[2,256,8,128]{3,2,1,0:T(8,128)(2,1)S(1)}, bf16[2,256,8,128]{3,2,1,0:T(8,128)(2,1)}, u32[]{:S(2)}) copy-start(bf16[2,256,8,128]{3,2,1,0:T(8,128)(2,1)} %param.19) | copy-start | bytes 3145732
  8.3 16.4 %copy-start.6 = (s32[4]{0:T(128)S(1)}, s32[4]{0:T(128)}, u32[]{:S(2)}) copy-start(s32[4]{0:T(128)} %order.3) | copy-start | bytes 52
  8.4 16.4 %copy-start.7 = (s32[4]{0:T(128)S(1)}, s32[4]{0:T(128)}, u32[]{:S(2)}) copy-start(s32[4]{0:T(128)} %stale.1) | copy-start | bytes 52
  8.4 16.4 %copy-start.8 = (s32[2]{0:T(128)S(1)}, s32[2]{0:T(128)}, u32[]{:S(2)}) copy-start(s32[2]{0:T(128)} %lengths.1) | copy-start | bytes 28
  26.8 5.7 %collective-permute-start.3 = (f32[48,128]{1,0:T(8,128)S(1)}, f32[48,128]{1,0:T(8,128)S(1)}, u32[]{:S(2)}, u32[]{:S(2)}) collective-permute-start(f32[48,128]{1,0:T(8,128)S(1)} %get-tuple-element.10), channel_id=1, source_target_pairs={{0,3},{1,2},{2,1},{3,0},{4,7},{5,6},{6,5},{7,4},{8,11},{9,10},{10,... | collective-permute-start | bytes 73736 | tf_op jit(solution)/shard_map/ppermute | solution.py:385
  28.2 4.9 %collective-permute-start.4 = (f32[48,128]{1,0:T(8,128)S(1)}, f32[48,128]{1,0:T(8,128)S(1)}, u32[]{:S(2)}, u32[]{:S(2)}) collective-permute-start(f32[48,128]{1,0:T(8,128)S(1)} %get-tuple-element.11), channel_id=1, source_target_pairs={{0,2},{1,3},{2,0},{3,1},{4,6},{5,7},{6,4},{7,5},{8,10},{9,11},{10,... | collective-permute-start | bytes 73736 | tf_op jit(solution)/shard_map/ppermute | solution.py:385
  29.5 3.9 %collective-permute-start.5 = (f32[48,128]{1,0:T(8,128)S(1)}, f32[48,128]{1,0:T(8,128)S(1)}, u32[]{:S(2)}, u32[]{:S(2)}) collective-permute-start(f32[48,128]{1,0:T(8,128)S(1)} %get-tuple-element.12), channel_id=1, source_target_pairs={{0,1},{1,0},{2,3},{3,2},{4,5},{5,4},{6,7},{7,6},{8,9},{9,8},{10,11... | collective-permute-start | bytes 73736 | tf_op jit(solution)/shard_map/ppermute | solution.py:385

commit v4 on v3

--- a/solution.py
+++ b/solution.py
@@ -93,6 +93,7 @@
 PROJECT_LIMIT = 24_000_000
 START_BYTES = 32 << 20
 SPANS = 4
+NEVER = -1e30
 
 
 def whole_block(space):
@@ -220,7 +221,10 @@
                 total = jnp.where(lane == g, pltpu.roll(sums[g], (step * (g - h)) % head_size, 1), total)
         turned[h * block : (h + 1) * block, :] = total
     lanes = lax.broadcasted_iota(jnp.int32, (SUBLANES, places), 1)
-    stats_lane = lax.broadcasted_iota(jnp.int32, (1, LANES), 1) // (LANES // (2 * rows_here))
+    head_of = lanes % kv_heads
+    place_of = mp * (places // kv_heads) + lanes // kv_heads
+    fields = 2 * rows_here
+    stats_lane = lax.broadcasted_iota(jnp.int32, (1, LANES), 1) // (LANES // fields)
     stats = [jnp.zeros((per_group, LANES), jnp.float32) for _ in range(kv_heads)]
     for i in range(rows_here):
         flag = jnp.int32(0)
@@ -249,24 +253,23 @@
 
         query = queries[i * head_count : (i + 1) * head_count, :].astype(jnp.bfloat16)
         fresh = slots[i * 2 * kv_heads : (i + 1) * 2 * kv_heads, :].astype(jnp.bfloat16).astype(jnp.float32)
-        scores = lax.dot_general(query, keys[i], (((1,), (1,)), ((), ())), preferred_element_type=jnp.float32) * scale
-        position = mp * (places // kv_heads) + lanes // kv_heads
-        valid = position < lengths[i]
-        weights, tops, totals, added = [], [], [], []
+        scores = lax.dot_general(query, keys[i], (((1,), (1,)), ((), ())), preferred_element_type=jnp.float32)
+        head_here = jnp.where(place_of < lengths[i], head_of, -1)
+        weights, added = [], []
         for b in range(kv_heads):
             span = slice(b * per_group, (b + 1) * per_group)
-            allowed = valid & (lanes % kv_heads == b)
-            mine = jnp.sum(query[span].astype(jnp.float32) * fresh[b : b + 1], axis=1, keepdims=True) * scale
-            mine = jnp.where(mp == 0, mine, -1e30)
-            top = jnp.max(jnp.where(allowed, scores[span], -1e30), axis=1, keepdims=True)
-            top = jnp.maximum(top, mine)
-            probable = jnp.where(allowed, jnp.exp(scores[span] - top), 0.0)
-            own = jnp.where(mp == 0, jnp.exp(mine - top), 0.0)
+            mine = jnp.sum(query[span].astype(jnp.float32) * fresh[b : b + 1], axis=1, keepdims=True)
+            mine = jnp.where(mp == 0, mine, NEVER)
+            held_scores = jnp.where(head_here == b, scores[span], NEVER)
+            top = jnp.maximum(jnp.max(held_scores, axis=1, keepdims=True), mine)
+            base = jnp.where(top == NEVER, 0.0, top)
+            probable = jnp.exp2((held_scores - base) * scale)
+            own = jnp.exp2((mine - base) * scale)
             total = jnp.sum(probable, axis=1, keepdims=True) + own
             weights.append(probable)
             added.append(own * fresh[kv_heads + b : kv_heads + b + 1])
-            stats[b] = jnp.where(stats_lane == 2 * i, top, stats[b])
-            stats[b] = jnp.where(stats_lane == 2 * i + 1, total, stats[b])
+            for n, value in enumerate((top, total)):
+                stats[b] = jnp.where(stats_lane == 2 * i + n, value, stats[b])
         weight = jnp.concatenate(weights, axis=0).astype(jnp.bfloat16)
         out = jnp.dot(weight, values[i], preferred_element_type=jnp.float32) + jnp.concatenate(added, axis=0)
         for m in range(n_mp):
@@ -278,18 +281,22 @@
         ref[...] = packed[jnp.bitwise_xor(mp, k)]
 
 
-def join_kernel(*refs):
+def join_kernel(scale, *refs):
     parts, out = refs[:-1], refs[-1]
     rows_here, heads_here, head_size = out.shape
     step = LANES // (2 * rows_here)
-    stats = rows_here * heads_here
+    values = [p[...] for p in parts]
+    stats = [v[rows_here * heads_here :, :] for v in values]
+
+    def field(block, n):
+        return block[:, n * step : n * step + 1]
+
     for i in range(rows_here):
-        tops = [p[stats:, 2 * i * step : 2 * i * step + 1] for p in parts]
-        sums = [p[stats:, (2 * i + 1) * step : (2 * i + 1) * step + 1] for p in parts]
+        tops = [field(block, 2 * i) for block in stats]
         joined = functools.reduce(jnp.maximum, tops)
-        scales = [jnp.exp(top - joined) for top in tops]
-        numerator = sum(p[i * heads_here : (i + 1) * heads_here, :] * s for p, s in zip(parts, scales))
-        divisor = sum(n * s for n, s in zip(sums, scales))
+        scales = [jnp.exp2((top - joined) * scale) for top in tops]
+        numerator = sum(v[i * heads_here : (i + 1) * heads_here, :] * s for v, s in zip(values, scales))
+        divisor = sum(field(block, 2 * i + 1) * s for block, s in zip(stats, scales))
         out[i] = (numerator / divisor).astype(out.dtype)
 
 
@@ -359,8 +366,9 @@
     held = held.reshape(n_grp * n_rep, block, head_size)
     places = positions_here * kv_heads
     packed_rows = (rows_here + 1) * heads_here
+    scale = math.log2(math.e) / math.sqrt(head_size)
     partial_out = pl.pallas_call(
-        functools.partial(attend_kernel, sizes, 1.0 / math.sqrt(head_size)),
+        functools.partial(attend_kernel, sizes, scale),
         out_shape=[f32((packed_rows, LANES))] * n_mp,
         in_specs=[whole_block(SMEM)] * 3 + [whole_block(VMEM)] * 3,
         out_specs=[whole_block(VMEM)] * n_mp,
@@ -385,7 +393,7 @@
         lax.ppermute(partial_out[k], "mp", [(i, i ^ k) for i in range(n_mp)]) for k in range(n_mp - 1, 0, -1)
     ]
     return pl.pallas_call(
-        join_kernel,
+        functools.partial(join_kernel, scale),
         out_shape=bf16((rows_here, heads_here, head_size)),
         in_specs=[whole_block(VMEM)] * n_mp,
         out_specs=whole_block(VMEM),
@@ -410,7 +418,7 @@
         and heads_here % SUBLANES == 0
         and slots_here * n_mp == 2 * kv_heads
         and n_mp * rows_here * (n_grp + 1) % SUBLANES == 0
-        and LANES % (2 * rows_here) == 0
+        and LANES // (2 * rows_here) > 0
         and n_grp * n_rep * rows_here % (2 * SUBLANES) == 0
         and old_q.shape[0] % (2 * SPANS * LANES) == 0
     )

time: 34.3 us -> 34.2 us (level)
  no operation moved by 1% of the time
where the time goes in v4:
time: 34.2 us; the launch traced here: 34 us
  blocking collectives  13.2 us (39%)
  Pallas kernels  9.58 us (28%)
  starting transfers between devices  7.64 us (22%)
  waiting for transfers between devices  3.42 us (10%)
    all_to_all x1, blocking collectives, close(): lax.all_to_all(terms.reshape(devices, 1, rows_here * parts * head_size),...  13.2 us
    ppermute x3, starting transfers between devices, close(): lax.ppermute(partial_out[k], 'mp', [(i, i ^ k) for i in range(n_mp)])  4.45 us
    ppermute x3, starting transfers between devices, exchanged(): lax.ppermute(value, axis, [(i, i ^ k) for i in range(count)])  3.19 us
    pallas_call x1, Pallas kernels, close(): pl.pallas_call(functools.partial(project_kernel, n_rep, n_mp), out_shape=...  3.07 us
    pallas_call x1, Pallas kernels, close(): pl.pallas_call(load_kernel, out_shape=bf16((part_width, shares, head_size...  2.21 us
    ppermute x3, waiting for transfers between devices, close(): lax.ppermute(partial_out[k], 'mp', [(i, i ^ k) for i in range(n_mp)])  2.13 us
    pallas_call x1, Pallas kernels, close(): pl.pallas_call(functools.partial(attend_kernel, sizes, scale), out_shape=...  1.94 us
    pallas_call x1, Pallas kernels, close(): pl.pallas_call(order_kernel, out_shape=bf16((group_rows, part_width + LAN...  1.6 us
  transfers between devices with their start and end apart: 6, of which 4 were waited for; matrix products, arithmetic and copies ran while one was open for 0% of the time, Pallas kernels for 6%

profile of v4, /device:TPU:0, one launch (start us, length us, event | category | flops | bytes accessed | tf_op | source)
XLA Modules:
  0.0 34.0 jit_solution(2263088062704510)
XLA Ops:
  0.0 0.0 copy-start.2
  0.0 1.6 %order.2.refs_0_ = bf16[4,4224]{1,0:T(4,128)(2,1)} custom-call(s32[4]{0:T(128)} %order.3, s32[4]{0:T(128)} %stale.1, bf16[4,4096]{1,0:T(4,128)(2,1)} %rows_in.1, bf16[4096,16,128]{2,1,0:T(8,128)(2,1)} %_.1), custom_call_target="tpu_custom_call" | custom-call | bytes 33554432 | tf_op jit(solution)/shard_map/order/pallas_call | solution.py:321
  1.6 2.5 %collective-permute-start.2 = (bf16[4,4224]{1,0:T(4,128)(2,1)}, bf16[4,4224]{1,0:T(4,128)(2,1)S(1)}, u32[]{:S(2)}, u32[]{:S(2)}) collective-permute-start(bf16[4,4224]{1,0:T(4,128)(2,1)} %order.2.refs_0_), channel_id=1, source_target_pairs={{0,24},{8,16},{16,8},{24,0},{1,25},{9,17},{17,9},{25,1},{2,26},{10... | collective-permute-start | bytes 101384 | tf_op jit(solution)/shard_map/ppermute | solution.py:304
  4.1 0.6 %collective-permute-start.1 = (bf16[4,4224]{1,0:T(4,128)(2,1)}, bf16[4,4224]{1,0:T(4,128)(2,1)S(1)}, u32[]{:S(2)}, u32[]{:S(2)}) collective-permute-start(bf16[4,4224]{1,0:T(4,128)(2,1)} %order.2.refs_0_), channel_id=1, source_target_pairs={{0,16},{8,24},{16,0},{24,8},{1,17},{9,25},{17,1},{25,9},{2,18},{10... | collective-permute-start | bytes 101384 | tf_op jit(solution)/shard_map/ppermute | solution.py:304
  4.8 0.0 collective-permute-start
  4.8 0.0 copy-done.2
  4.8 0.0 copy-done.1
  4.8 0.0 copy-done
  4.8 2.2 %load.1 = bf16[4096,4,128]{2,1,0:T(4,128)(2,1)S(1)} custom-call(bf16[4096,4,4,128]{3,2,1,0:T(4,128)(2,1)} %bitcast.24, bf16[16384,128]{1,0:T(8,128)(2,1)S(1)} %bitcast.13, bf16[512,4096]{1,0:T(8,128)(2,1)S(1)} %bitcast.15, bf16[128,4096]{1,0:T(8,128)(2,1)S(1)} %bitcast.18), custom_call_target="tpu_custom_call" | custom-call | tf_op jit(solution)/shard_map/load/pallas_call | solution.py:342
  7.0 0.0 collective-permute-done.2.refs_3_
  7.0 1.3 %collective-permute-done.1.refs_2_ = bf16[4,4224]{1,0:T(4,128)(2,1)S(1)} collective-permute-done((bf16[4,4224]{1,0:T(4,128)(2,1)}, bf16[4,4224]{1,0:T(4,128)(2,1)S(1)}, u32[]{:S(2)}, u32[]{:S(2)}) %collective-permute-start.1) | collective-permute-done | bytes 33824 | tf_op jit(solution)/shard_map/ppermute | solution.py:304
  8.3 0.0 collective-permute-done.refs_1_
  8.3 0.0 copy-done.5
  8.3 0.0 copy-start.4
  8.3 0.0 copy-start.6
  8.4 0.0 copy-start.7
  8.4 0.0 copy-start.8
  8.4 3.1 %project.1 = f32[8,40,128]{2,1,0:T(8,128)S(1)} custom-call(bf16[4,4224]{1,0:T(4,128)(2,1)S(1)} %copy-done.5, bf16[4,4224]{1,0:T(4,128)(2,1)S(1)} %collective-permute-done.refs_1_, bf16[4,4224]{1,0:T(4,128)(2,1)S(1)} %collective-permute-done.1.refs_2_, bf16[4,4224]{1,0:T(4,128)(2,1)S(1)} %collective-permute-done.2.refs_3_, bf16[16384,128]{1,0:T(8,128)(2,1)S(1)} %bitcast.17, ...), custom_call_target="tpu_custom_call" | custom-call | tf_op jit(solution)/shard_map/project/pallas_call | solution.py:352
  11.5 13.2 %all_to_all.5 = f32[32,1,1280]{2,1,0:T(1,128)S(1)} all-to-all(f32[32,1,1280]{2,1,0:T(1,128)S(1)} %bitcast.23), channel_id=1, replica_groups=mesh['grp'=4,'rep'=2,'mp'=4] {'grp','rep','mp'}, dimensions={0} | all-to-all | bytes 327680 | tf_op jit(solution)/shard_map/all_to_all | solution.py:365
  24.7 0.0 copy-done.3
  24.7 0.0 copy-done.4
  24.7 0.0 copy-done.6
  24.7 0.0 copy-done.7
  24.7 0.0 copy-done.8
  24.7 1.9 %attend.1 = (f32[48,128]{1,0:T(8,128)S(1)}, f32[48,128]{1,0:T(8,128)S(1)}, f32[48,128]{1,0:T(8,128)S(1)}, f32[48,128]{1,0:T(8,128)S(1)}) custom-call(s32[4]{0:T(128)S(1)} %copy-done.6, s32[4]{0:T(128)S(1)} %copy-done.7, s32[2]{0:T(128)S(1)} %copy-done.8, f32[8,40,128]{2,1,0:T(8,128)S(1)} %bitcast.22, bf16[2,2048,128]{2,1,0:T(8,128)(2,1)S(1)} %bitcast.20, ...), custom_call_target="tpu_custom_call" | custom-call | tf_op jit(solution)/shard_map/attend/pallas_call | solution.py:370
  26.7 1.4 %collective-permute-start.3 = (f32[48,128]{1,0:T(8,128)S(1)}, f32[48,128]{1,0:T(8,128)S(1)}, u32[]{:S(2)}, u32[]{:S(2)}) collective-permute-start(f32[48,128]{1,0:T(8,128)S(1)} %get-tuple-element.10), channel_id=1, source_target_pairs={{0,3},{1,2},{2,1},{3,0},{4,7},{5,6},{6,5},{7,4},{8,11},{9,10},{10,... | collective-permute-start | bytes 73736 | tf_op jit(solution)/shard_map/ppermute | solution.py:393
  28.1 1.3 %collective-permute-start.4 = (f32[48,128]{1,0:T(8,128)S(1)}, f32[48,128]{1,0:T(8,128)S(1)}, u32[]{:S(2)}, u32[]{:S(2)}) collective-permute-start(f32[48,128]{1,0:T(8,128)S(1)} %get-tuple-element.11), channel_id=1, source_target_pairs={{0,2},{1,3},{2,0},{3,1},{4,6},{5,7},{6,4},{7,5},{8,10},{9,11},{10,... | collective-permute-start | bytes 73736 | tf_op jit(solution)/shard_map/ppermute | solution.py:393
  29.4 1.7 %collective-permute-start.5 = (f32[48,128]{1,0:T(8,128)S(1)}, f32[48,128]{1,0:T(8,128)S(1)}, u32[]{:S(2)}, u32[]{:S(2)}) collective-permute-start(f32[48,128]{1,0:T(8,128)S(1)} %get-tuple-element.12), channel_id=1, source_target_pairs={{0,1},{1,0},{2,3},{3,2},{4,5},{5,4},{6,7},{7,6},{8,9},{9,8},{10,11... | collective-permute-start | bytes 73736 | tf_op jit(solution)/shard_map/ppermute | solution.py:393
  31.1 1.2 %collective-permute-done.3.refs_1_ = f32[48,128]{1,0:T(8,128)S(1)} collective-permute-done((f32[48,128]{1,0:T(8,128)S(1)}, f32[48,128]{1,0:T(8,128)S(1)}, u32[]{:S(2)}, u32[]{:S(2)}) %collective-permute-start.3) | collective-permute-done | bytes 24608 | tf_op jit(solution)/shard_map/ppermute | solution.py:393
  32.4 0.7 %collective-permute-done.4.refs_2_ = f32[48,128]{1,0:T(8,128)S(1)} collective-permute-done((f32[48,128]{1,0:T(8,128)S(1)}, f32[48,128]{1,0:T(8,128)S(1)}, u32[]{:S(2)}, u32[]{:S(2)}) %collective-permute-start.4) | collective-permute-done | bytes 24608 | tf_op jit(solution)/shard_map/ppermute | solution.py:393
  33.0 0.2 collective-permute-done.5.refs_3_
  33.3 0.8 %join.1 = bf16[2,16,128]{2,1,0:T(8,128)(2,1)} custom-call(f32[48,128]{1,0:T(8,128)S(1)} %get-tuple-element.9.refs_0_, f32[48,128]{1,0:T(8,128)S(1)} %collective-permute-done.3.refs_1_, f32[48,128]{1,0:T(8,128)S(1)} %collective-permute-done.4.refs_2_, f32[48,128]{1,0:T(8,128)S(1)} %collective-permute-done.5.refs_3_), custom_call_target="tpu_custom_call" | custom-call | tf_op jit(solution)/shard_map/join/pallas_call | solution.py:395
  (4 shorter events, 0.0 us)
Async XLA Ops:
  0.0 4.8 %copy-start.2 = (bf16[4096,4,32]{0,2,1:T(8,128)(2,1)S(1)}, bf16[4096,4,32]{0,2,1:T(8,128)(2,1)}, u32[]{:S(2)}) copy-start(bf16[4096,4,32]{0,2,1:T(8,128)(2,1)} %param.17) | copy-start | bytes 3145732
  0.0 4.8 %copy-start.1 = (bf16[4096,16,32]{0,2,1:T(8,128)(2,1)S(1)}, bf16[4096,16,32]{0,2,1:T(8,128)(2,1)}, u32[]{:S(2)}) copy-start(bf16[4096,16,32]{0,2,1:T(8,128)(2,1)} %param.16) | copy-start | bytes 12582916
  0.0 4.8 %copy-start = (bf16[4096,4,128]{2,1,0:T(4,128)(2,1)S(1)}, bf16[4096,4,128]{2,1,0:T(4,128)(2,1)}, u32[]{:S(2)}) copy-start(bf16[4096,4,128]{2,1,0:T(4,128)(2,1)} %param.15) | copy-start | bytes 12582916
  1.6 5.4 %collective-permute-start.2 = (bf16[4,4224]{1,0:T(4,128)(2,1)}, bf16[4,4224]{1,0:T(4,128)(2,1)S(1)}, u32[]{:S(2)}, u32[]{:S(2)}) collective-permute-start(bf16[4,4224]{1,0:T(4,128)(2,1)} %order.2.refs_0_), channel_id=1, source_target_pairs={{0,24},{8,16},{16,8},{24,0},{1,25},{9,17},{17,9},{25,1},{2,26},{10... | collective-permute-start | bytes 101384 | tf_op jit(solution)/shard_map/ppermute | solution.py:304
  4.1 4.2 %collective-permute-start.1 = (bf16[4,4224]{1,0:T(4,128)(2,1)}, bf16[4,4224]{1,0:T(4,128)(2,1)S(1)}, u32[]{:S(2)}, u32[]{:S(2)}) collective-permute-start(bf16[4,4224]{1,0:T(4,128)(2,1)} %order.2.refs_0_), channel_id=1, source_target_pairs={{0,16},{8,24},{16,0},{24,8},{1,17},{9,25},{17,1},{25,9},{2,18},{10... | collective-permute-start | bytes 101384 | tf_op jit(solution)/shard_map/ppermute | solution.py:304
  4.8 3.6 %collective-permute-start = (bf16[4,4224]{1,0:T(4,128)(2,1)}, bf16[4,4224]{1,0:T(4,128)(2,1)S(1)}, u32[]{:S(2)}, u32[]{:S(2)}) collective-permute-start(bf16[4,4224]{1,0:T(4,128)(2,1)} %order.2.refs_0_), channel_id=1, source_target_pairs={{0,8},{8,0},{16,24},{24,16},{1,9},{9,1},{17,25},{25,17},{2,10},{10... | collective-permute-start | bytes 101384 | tf_op jit(solution)/shard_map/ppermute | solution.py:304
  4.8 3.5 %copy-start.5 = (bf16[4,4224]{1,0:T(4,128)(2,1)S(1)}, bf16[4,4224]{1,0:T(4,128)(2,1)}, u32[]{:S(2)}) copy-start(bf16[4,4224]{1,0:T(4,128)(2,1)} %order.2.refs_0_) | copy-start | bytes 101380
  8.3 16.4 %copy-start.3 = (bf16[2,256,8,128]{3,2,1,0:T(8,128)(2,1)S(1)}, bf16[2,256,8,128]{3,2,1,0:T(8,128)(2,1)}, u32[]{:S(2)}) copy-start(bf16[2,256,8,128]{3,2,1,0:T(8,128)(2,1)} %param.18) | copy-start | bytes 3145732
  8.3 16.4 %copy-start.4 = (bf16[2,256,8,128]{3,2,1,0:T(8,128)(2,1)S(1)}, bf16[2,256,8,128]{3,2,1,0:T(8,128)(2,1)}, u32[]{:S(2)}) copy-start(bf16[2,256,8,128]{3,2,1,0:T(8,128)(2,1)} %param.19) | copy-start | bytes 3145732
  8.3 16.4 %copy-start.6 = (s32[4]{0:T(128)S(1)}, s32[4]{0:T(128)}, u32[]{:S(2)}) copy-start(s32[4]{0:T(128)} %order.3) | copy-start | bytes 52
  8.4 16.4 %copy-start.7 = (s32[4]{0:T(128)S(1)}, s32[4]{0:T(128)}, u32[]{:S(2)}) copy-start(s32[4]{0:T(128)} %stale.1) | copy-start | bytes 52
  8.4 16.4 %copy-start.8 = (s32[2]{0:T(128)S(1)}, s32[2]{0:T(128)}, u32[]{:S(2)}) copy-start(s32[2]{0:T(128)} %lengths.1) | copy-start | bytes 28
  26.7 5.7 %collective-permute-start.3 = (f32[48,128]{1,0:T(8,128)S(1)}, f32[48,128]{1,0:T(8,128)S(1)}, u32[]{:S(2)}, u32[]{:S(2)}) collective-permute-start(f32[48,128]{1,0:T(8,128)S(1)} %get-tuple-element.10), channel_id=1, source_target_pairs={{0,3},{1,2},{2,1},{3,0},{4,7},{5,6},{6,5},{7,4},{8,11},{9,10},{10,... | collective-permute-start | bytes 73736 | tf_op jit(solution)/shard_map/ppermute | solution.py:393
  28.1 4.9 %collective-permute-start.4 = (f32[48,128]{1,0:T(8,128)S(1)}, f32[48,128]{1,0:T(8,128)S(1)}, u32[]{:S(2)}, u32[]{:S(2)}) collective-permute-start(f32[48,128]{1,0:T(8,128)S(1)} %get-tuple-element.11), channel_id=1, source_target_pairs={{0,2},{1,3},{2,0},{3,1},{4,6},{5,7},{6,4},{7,5},{8,10},{9,11},{10,... | collective-permute-start | bytes 73736 | tf_op jit(solution)/shard_map/ppermute | solution.py:393
  29.4 3.9 %collective-permute-start.5 = (f32[48,128]{1,0:T(8,128)S(1)}, f32[48,128]{1,0:T(8,128)S(1)}, u32[]{:S(2)}, u32[]{:S(2)}) collective-permute-start(f32[48,128]{1,0:T(8,128)S(1)} %get-tuple-element.12), channel_id=1, source_target_pairs={{0,1},{1,0},{2,3},{3,2},{4,5},{5,4},{6,7},{7,6},{8,9},{9,8},{10,11... | collective-permute-start | bytes 73736 | tf_op jit(solution)/shard_map/ppermute | solution.py:393

commit v5 on v4

--- a/solution.py
+++ b/solution.py
@@ -92,7 +92,7 @@
 LOAD_LIMIT = 40_000_000
 PROJECT_LIMIT = 24_000_000
 START_BYTES = 32 << 20
-SPANS = 4
+SPANS = 16
 NEVER = -1e30
 
 

time: 34.2 us -> 34.3 us (level)
  no operation moved by 1% of the time
where the time goes in v5:
time: 34.3 us; the launch traced here: 34.1 us
  blocking collectives  13.2 us (38%)
  Pallas kernels  9.66 us (28%)
  starting transfers between devices  7.64 us (22%)
  waiting for transfers between devices  3.42 us (10%)
    all_to_all x1, blocking collectives, close(): lax.all_to_all(terms.reshape(devices, 1, rows_here * parts * head_size),...  13.2 us
    ppermute x3, starting transfers between devices, close(): lax.ppermute(partial_out[k], 'mp', [(i, i ^ k) for i in range(n_mp)])  4.45 us
    ppermute x3, starting transfers between devices, exchanged(): lax.ppermute(value, axis, [(i, i ^ k) for i in range(count)])  3.19 us
    pallas_call x1, Pallas kernels, close(): pl.pallas_call(functools.partial(project_kernel, n_rep, n_mp), out_shape=...  3.14 us
    pallas_call x1, Pallas kernels, close(): pl.pallas_call(load_kernel, out_shape=bf16((part_width, shares, head_size...  2.21 us
    ppermute x3, waiting for transfers between devices, close(): lax.ppermute(partial_out[k], 'mp', [(i, i ^ k) for i in range(n_mp)])  2.13 us
    pallas_call x1, Pallas kernels, close(): pl.pallas_call(functools.partial(attend_kernel, sizes, scale), out_shape=...  1.95 us
    pallas_call x1, Pallas kernels, close(): pl.pallas_call(order_kernel, out_shape=bf16((group_rows, part_width + LAN...  1.6 us
  transfers between devices with their start and end apart: 6, of which 4 were waited for; matrix products, arithmetic and copies ran while one was open for 0% of the time, Pallas kernels for 6%

profile of v5, /device:TPU:0, one launch (start us, length us, event | category | flops | bytes accessed | tf_op | source)
XLA Modules:
  0.0 34.1 jit_solution(17484352420752655249)
XLA Ops:
  0.0 0.0 copy-start.1
  0.0 1.6 %order.2.refs_0_ = bf16[4,4224]{1,0:T(4,128)(2,1)} custom-call(s32[4]{0:T(128)} %order.3, s32[4]{0:T(128)} %stale.1, bf16[4,4096]{1,0:T(4,128)(2,1)} %rows_in.1, bf16[4096,16,128]{2,1,0:T(8,128)(2,1)} %_.1), custom_call_target="tpu_custom_call" | custom-call | bytes 33554432 | tf_op jit(solution)/shard_map/order/pallas_call | solution.py:321
  1.6 2.5 %collective-permute-start.2 = (bf16[4,4224]{1,0:T(4,128)(2,1)}, bf16[4,4224]{1,0:T(4,128)(2,1)S(1)}, u32[]{:S(2)}, u32[]{:S(2)}) collective-permute-start(bf16[4,4224]{1,0:T(4,128)(2,1)} %order.2.refs_0_), channel_id=1, source_target_pairs={{0,24},{8,16},{16,8},{24,0},{1,25},{9,17},{17,9},{25,1},{2,26},{10... | collective-permute-start | bytes 101384 | tf_op jit(solution)/shard_map/ppermute | solution.py:304
  4.1 0.6 %collective-permute-start.1 = (bf16[4,4224]{1,0:T(4,128)(2,1)}, bf16[4,4224]{1,0:T(4,128)(2,1)S(1)}, u32[]{:S(2)}, u32[]{:S(2)}) collective-permute-start(bf16[4,4224]{1,0:T(4,128)(2,1)} %order.2.refs_0_), channel_id=1, source_target_pairs={{0,16},{8,24},{16,0},{24,8},{1,17},{9,25},{17,1},{25,9},{2,18},{10... | collective-permute-start | bytes 101384 | tf_op jit(solution)/shard_map/ppermute | solution.py:304
  4.8 0.0 collective-permute-start
  4.8 0.0 copy-done.2
  4.8 0.0 copy-done.1
  4.8 0.0 copy-done
  4.8 2.2 %load.1 = bf16[4096,4,128]{2,1,0:T(4,128)(2,1)S(1)} custom-call(bf16[4096,4,4,128]{3,2,1,0:T(4,128)(2,1)} %bitcast.24, bf16[16384,128]{1,0:T(8,128)(2,1)S(1)} %bitcast.13, bf16[512,4096]{1,0:T(8,128)(2,1)S(1)} %bitcast.15, bf16[128,4096]{1,0:T(8,128)(2,1)S(1)} %bitcast.18), custom_call_target="tpu_custom_call" | custom-call | tf_op jit(solution)/shard_map/load/pallas_call | solution.py:342
  7.0 0.0 collective-permute-done.2.refs_3_
  7.0 1.3 %collective-permute-done.1.refs_2_ = bf16[4,4224]{1,0:T(4,128)(2,1)S(1)} collective-permute-done((bf16[4,4224]{1,0:T(4,128)(2,1)}, bf16[4,4224]{1,0:T(4,128)(2,1)S(1)}, u32[]{:S(2)}, u32[]{:S(2)}) %collective-permute-start.1) | collective-permute-done | bytes 33824 | tf_op jit(solution)/shard_map/ppermute | solution.py:304
  8.3 0.0 collective-permute-done.refs_1_
  8.3 0.0 copy-done.5
  8.3 0.0 copy-start.4
  8.3 0.0 copy-start.6
  8.4 0.0 copy-start.7
  8.4 0.0 copy-start.8
  8.4 3.1 %project.1 = f32[8,40,128]{2,1,0:T(8,128)S(1)} custom-call(bf16[4,4224]{1,0:T(4,128)(2,1)S(1)} %copy-done.5, bf16[4,4224]{1,0:T(4,128)(2,1)S(1)} %collective-permute-done.refs_1_, bf16[4,4224]{1,0:T(4,128)(2,1)S(1)} %collective-permute-done.1.refs_2_, bf16[4,4224]{1,0:T(4,128)(2,1)S(1)} %collective-permute-done.2.refs_3_, bf16[16384,128]{1,0:T(8,128)(2,1)S(1)} %bitcast.17, ...), custom_call_target="tpu_custom_call" | custom-call | tf_op jit(solution)/shard_map/project/pallas_call | solution.py:352
  11.5 13.2 %all_to_all.5 = f32[32,1,1280]{2,1,0:T(1,128)S(1)} all-to-all(f32[32,1,1280]{2,1,0:T(1,128)S(1)} %bitcast.23), channel_id=1, replica_groups=mesh['grp'=4,'rep'=2,'mp'=4] {'grp','rep','mp'}, dimensions={0} | all-to-all | bytes 327680 | tf_op jit(solution)/shard_map/all_to_all | solution.py:365
  24.8 0.0 copy-done.3
  24.8 0.0 copy-done.4
  24.8 0.0 copy-done.6
  24.8 0.0 copy-done.7
  24.8 0.0 copy-done.8
  24.8 2.0 %attend.1 = (f32[48,128]{1,0:T(8,128)S(1)}, f32[48,128]{1,0:T(8,128)S(1)}, f32[48,128]{1,0:T(8,128)S(1)}, f32[48,128]{1,0:T(8,128)S(1)}) custom-call(s32[4]{0:T(128)S(1)} %copy-done.6, s32[4]{0:T(128)S(1)} %copy-done.7, s32[2]{0:T(128)S(1)} %copy-done.8, f32[8,40,128]{2,1,0:T(8,128)S(1)} %bitcast.22, bf16[2,2048,128]{2,1,0:T(8,128)(2,1)S(1)} %bitcast.20, ...), custom_call_target="tpu_custom_call" | custom-call | tf_op jit(solution)/shard_map/attend/pallas_call | solution.py:370
  26.8 1.4 %collective-permute-start.3 = (f32[48,128]{1,0:T(8,128)S(1)}, f32[48,128]{1,0:T(8,128)S(1)}, u32[]{:S(2)}, u32[]{:S(2)}) collective-permute-start(f32[48,128]{1,0:T(8,128)S(1)} %get-tuple-element.10), channel_id=1, source_target_pairs={{0,3},{1,2},{2,1},{3,0},{4,7},{5,6},{6,5},{7,4},{8,11},{9,10},{10,... | collective-permute-start | bytes 73736 | tf_op jit(solution)/shard_map/ppermute | solution.py:393
  28.2 1.3 %collective-permute-start.4 = (f32[48,128]{1,0:T(8,128)S(1)}, f32[48,128]{1,0:T(8,128)S(1)}, u32[]{:S(2)}, u32[]{:S(2)}) collective-permute-start(f32[48,128]{1,0:T(8,128)S(1)} %get-tuple-element.11), channel_id=1, source_target_pairs={{0,2},{1,3},{2,0},{3,1},{4,6},{5,7},{6,4},{7,5},{8,10},{9,11},{10,... | collective-permute-start | bytes 73736 | tf_op jit(solution)/shard_map/ppermute | solution.py:393
  29.5 1.7 %collective-permute-start.5 = (f32[48,128]{1,0:T(8,128)S(1)}, f32[48,128]{1,0:T(8,128)S(1)}, u32[]{:S(2)}, u32[]{:S(2)}) collective-permute-start(f32[48,128]{1,0:T(8,128)S(1)} %get-tuple-element.12), channel_id=1, source_target_pairs={{0,1},{1,0},{2,3},{3,2},{4,5},{5,4},{6,7},{7,6},{8,9},{9,8},{10,11... | collective-permute-start | bytes 73736 | tf_op jit(solution)/shard_map/ppermute | solution.py:393
  31.2 1.2 %collective-permute-done.3.refs_1_ = f32[48,128]{1,0:T(8,128)S(1)} collective-permute-done((f32[48,128]{1,0:T(8,128)S(1)}, f32[48,128]{1,0:T(8,128)S(1)}, u32[]{:S(2)}, u32[]{:S(2)}) %collective-permute-start.3) | collective-permute-done | bytes 24608 | tf_op jit(solution)/shard_map/ppermute | solution.py:393
  32.5 0.7 %collective-permute-done.4.refs_2_ = f32[48,128]{1,0:T(8,128)S(1)} collective-permute-done((f32[48,128]{1,0:T(8,128)S(1)}, f32[48,128]{1,0:T(8,128)S(1)}, u32[]{:S(2)}, u32[]{:S(2)}) %collective-permute-start.4) | collective-permute-done | bytes 24608 | tf_op jit(solution)/shard_map/ppermute | solution.py:393
  33.1 0.2 collective-permute-done.5.refs_3_
  33.4 0.8 %join.1 = bf16[2,16,128]{2,1,0:T(8,128)(2,1)} custom-call(f32[48,128]{1,0:T(8,128)S(1)} %get-tuple-element.9.refs_0_, f32[48,128]{1,0:T(8,128)S(1)} %collective-permute-done.3.refs_1_, f32[48,128]{1,0:T(8,128)S(1)} %collective-permute-done.4.refs_2_, f32[48,128]{1,0:T(8,128)S(1)} %collective-permute-done.5.refs_3_), custom_call_target="tpu_custom_call" | custom-call | tf_op jit(solution)/shard_map/join/pallas_call | solution.py:395
  (4 shorter events, 0.0 us)
Async XLA Ops:
  0.0 4.8 %copy-start.2 = (bf16[4096,4,32]{0,2,1:T(8,128)(2,1)S(1)}, bf16[4096,4,32]{0,2,1:T(8,128)(2,1)}, u32[]{:S(2)}) copy-start(bf16[4096,4,32]{0,2,1:T(8,128)(2,1)} %param.17) | copy-start | bytes 3145732
  0.0 4.8 %copy-start.1 = (bf16[4096,16,32]{0,2,1:T(8,128)(2,1)S(1)}, bf16[4096,16,32]{0,2,1:T(8,128)(2,1)}, u32[]{:S(2)}) copy-start(bf16[4096,16,32]{0,2,1:T(8,128)(2,1)} %param.16) | copy-start | bytes 12582916
  0.0 4.8 %copy-start = (bf16[4096,4,128]{2,1,0:T(4,128)(2,1)S(1)}, bf16[4096,4,128]{2,1,0:T(4,128)(2,1)}, u32[]{:S(2)}) copy-start(bf16[4096,4,128]{2,1,0:T(4,128)(2,1)} %param.15) | copy-start | bytes 12582916
  1.6 5.4 %collective-permute-start.2 = (bf16[4,4224]{1,0:T(4,128)(2,1)}, bf16[4,4224]{1,0:T(4,128)(2,1)S(1)}, u32[]{:S(2)}, u32[]{:S(2)}) collective-permute-start(bf16[4,4224]{1,0:T(4,128)(2,1)} %order.2.refs_0_), channel_id=1, source_target_pairs={{0,24},{8,16},{16,8},{24,0},{1,25},{9,17},{17,9},{25,1},{2,26},{10... | collective-permute-start | bytes 101384 | tf_op jit(solution)/shard_map/ppermute | solution.py:304
  4.1 4.2 %collective-permute-start.1 = (bf16[4,4224]{1,0:T(4,128)(2,1)}, bf16[4,4224]{1,0:T(4,128)(2,1)S(1)}, u32[]{:S(2)}, u32[]{:S(2)}) collective-permute-start(bf16[4,4224]{1,0:T(4,128)(2,1)} %order.2.refs_0_), channel_id=1, source_target_pairs={{0,16},{8,24},{16,0},{24,8},{1,17},{9,25},{17,1},{25,9},{2,18},{10... | collective-permute-start | bytes 101384 | tf_op jit(solution)/shard_map/ppermute | solution.py:304
  4.8 3.6 %collective-permute-start = (bf16[4,4224]{1,0:T(4,128)(2,1)}, bf16[4,4224]{1,0:T(4,128)(2,1)S(1)}, u32[]{:S(2)}, u32[]{:S(2)}) collective-permute-start(bf16[4,4224]{1,0:T(4,128)(2,1)} %order.2.refs_0_), channel_id=1, source_target_pairs={{0,8},{8,0},{16,24},{24,16},{1,9},{9,1},{17,25},{25,17},{2,10},{10... | collective-permute-start | bytes 101384 | tf_op jit(solution)/shard_map/ppermute | solution.py:304
  4.8 3.5 %copy-start.5 = (bf16[4,4224]{1,0:T(4,128)(2,1)S(1)}, bf16[4,4224]{1,0:T(4,128)(2,1)}, u32[]{:S(2)}) copy-start(bf16[4,4224]{1,0:T(4,128)(2,1)} %order.2.refs_0_) | copy-start | bytes 101380
  8.3 16.4 %copy-start.3 = (bf16[2,256,8,128]{3,2,1,0:T(8,128)(2,1)S(1)}, bf16[2,256,8,128]{3,2,1,0:T(8,128)(2,1)}, u32[]{:S(2)}) copy-start(bf16[2,256,8,128]{3,2,1,0:T(8,128)(2,1)} %param.18) | copy-start | bytes 3145732
  8.3 16.4 %copy-start.4 = (bf16[2,256,8,128]{3,2,1,0:T(8,128)(2,1)S(1)}, bf16[2,256,8,128]{3,2,1,0:T(8,128)(2,1)}, u32[]{:S(2)}) copy-start(bf16[2,256,8,128]{3,2,1,0:T(8,128)(2,1)} %param.19) | copy-start | bytes 3145732
  8.3 16.4 %copy-start.6 = (s32[4]{0:T(128)S(1)}, s32[4]{0:T(128)}, u32[]{:S(2)}) copy-start(s32[4]{0:T(128)} %order.3) | copy-start | bytes 52
  8.4 16.4 %copy-start.7 = (s32[4]{0:T(128)S(1)}, s32[4]{0:T(128)}, u32[]{:S(2)}) copy-start(s32[4]{0:T(128)} %stale.1) | copy-start | bytes 52
  8.4 16.4 %copy-start.8 = (s32[2]{0:T(128)S(1)}, s32[2]{0:T(128)}, u32[]{:S(2)}) copy-start(s32[2]{0:T(128)} %lengths.1) | copy-start | bytes 28
  26.8 5.7 %collective-permute-start.3 = (f32[48,128]{1,0:T(8,128)S(1)}, f32[48,128]{1,0:T(8,128)S(1)}, u32[]{:S(2)}, u32[]{:S(2)}) collective-permute-start(f32[48,128]{1,0:T(8,128)S(1)} %get-tuple-element.10), channel_id=1, source_target_pairs={{0,3},{1,2},{2,1},{3,0},{4,7},{5,6},{6,5},{7,4},{8,11},{9,10},{10,... | collective-permute-start | bytes 73736 | tf_op jit(solution)/shard_map/ppermute | solution.py:393
  28.2 4.9 %collective-permute-start.4 = (f32[48,128]{1,0:T(8,128)S(1)}, f32[48,128]{1,0:T(8,128)S(1)}, u32[]{:S(2)}, u32[]{:S(2)}) collective-permute-start(f32[48,128]{1,0:T(8,128)S(1)} %get-tuple-element.11), channel_id=1, source_target_pairs={{0,2},{1,3},{2,0},{3,1},{4,6},{5,7},{6,4},{7,5},{8,10},{9,11},{10,... | collective-permute-start | bytes 73736 | tf_op jit(solution)/shard_map/ppermute | solution.py:393
  29.5 3.9 %collective-permute-start.5 = (f32[48,128]{1,0:T(8,128)S(1)}, f32[48,128]{1,0:T(8,128)S(1)}, u32[]{:S(2)}, u32[]{:S(2)}) collective-permute-start(f32[48,128]{1,0:T(8,128)S(1)} %get-tuple-element.12), channel_id=1, source_target_pairs={{0,1},{1,0},{2,3},{3,2},{4,5},{5,4},{6,7},{7,6},{8,9},{9,8},{10,11... | collective-permute-start | bytes 73736 | tf_op jit(solution)/shard_map/ppermute | solution.py:393
